TPU v7x, 512 devices: a whole 4x8x8 slice. The times are simulated.
512 devices in a mesh: dp: 32 (over z, x), rows: 16 (over y, core).
Axes of the slice: x: 4, y: 8, z: 8, core: 2. Of those that a mesh axis runs over, the one named last changes fastest.
Arguments:
- older_output: bfloat16 [7680, 12, 2048], P(('dp', 'rows')), parts along dimension 0, may hold values from -6 to 6
- newer_output: bfloat16 [7680, 12, 2048], P(('dp', 'rows')), parts along dimension 0, may hold values from -6 to 6
- output_grad: bfloat16 [7680, 12, 2048], P(('dp', 'rows')), parts along dimension 0, may hold values from -6 to 6
- older_weight: bfloat16 [2048, 512], P('rows'), may hold values from -0.1875 to 0.1875
- newer_weight: bfloat16 [2048, 512], P('rows'), may hold values from -0.1875 to 0.1875
- square_point: bfloat16 [512, 512], P('rows'), may hold values from -0.25 to 0.25
- column_point: bfloat16 [512, 512], P('rows'), may hold values from -0.25 to 0.25
- square_kernel: float32 [3, 3, 512], replicated, may hold values from -2.4 to 2.4
- column_kernel: float32 [7, 512], replicated, may hold values from -2.4 to 2.4
Outputs:
- cell_output: bfloat16 [7680, 12, 2048], P(('dp', 'rows')), parts along dimension 0
- older_grad: bfloat16 [7680, 12, 2048], P(('dp', 'rows')), parts along dimension 0
- newer_grad: bfloat16 [7680, 12, 2048], P(('dp', 'rows')), parts along dimension 0
There are 32 independent parts, one for each index of `dp`. A program takes and returns all parts, laid end to end along the dimension named above; an argument that names none is the same for every part. Nothing has to cross between parts.
All inputs are finite; a program needn't handle non-finite values.
Results may differ from a plain program's by a relative error of at most 0.0057.
Values may be sent and summed in bfloat16 or wider, within the bound.
No kernel may reach another device: no remote copies, remote signals or barrier semaphores. Data moves between devices by JAX's collectives and lax.ppermute only.
A program may use at most 64 MiB of HBM per device.

v0:
```python
import jax
import jax.numpy as jnp
from jax import lax
from jax.sharding import PartitionSpec as P

HEIGHT = 30


def with_halo(block, sides, width):
    for axis, dim in sides:
        count = lax.axis_size(axis)
        forward = [(i, i + 1) for i in range(count - 1)]
        backward = [(target, source) for source, target in forward]
        low = lax.ppermute(
            lax.slice_in_dim(block, block.shape[dim] - width, None, axis=dim), axis, forward
        )
        high = lax.ppermute(lax.slice_in_dim(block, 0, width, axis=dim), axis, backward)
        block = jnp.concatenate([low, block, high], axis=dim)
    return block


def same_image(first_row, local_rows, offset):
    row_ids = jnp.arange(local_rows, dtype=jnp.int32) + first_row
    inside = jnp.floor_divide(row_ids + offset, HEIGHT) == jnp.floor_divide(row_ids, HEIGHT)
    return jnp.where(inside, 1.0, 0.0).astype(jnp.float32)[:, None, None]


def square_taps(padded, kernel, flip, first_row):
    full = jnp.pad(padded, ((0, 0), (1, 1), (0, 0))).astype(jnp.float32)
    height = full.shape[0] - 2
    across = full.shape[1] - 2
    total = jnp.zeros((height, across, full.shape[2]), jnp.float32)
    for i in range(3):
        keep = same_image(first_row, height, (2 - i if flip else i) - 1)
        for j in range(3):
            first = 2 - i if flip else i
            second = 2 - j if flip else j
            total = total + full[first : first + height, second : second + across, :] * (
                kernel[i, j] * keep
            )
    return total


def column_taps(padded, kernel, flip, first_row):
    full = padded.astype(jnp.float32)
    height = full.shape[0] - 6
    total = jnp.zeros((height, full.shape[1], full.shape[2]), jnp.float32)
    for i in range(7):
        first = 6 - i if flip else i
        keep = same_image(first_row, height, first - 3)
        total = total + full[first : first + height, :, :] * (kernel[i] * keep)
    return total


def local(
    older_output,
    newer_output,
    output_grad,
    older_weight,
    newer_weight,
    square_point,
    column_point,
    square_kernel,
    column_kernel,
):
    height, across, channels = older_output.shape
    filters = square_point.shape[1]
    shape_three = (height, across, filters)
    first_row = lax.axis_index("rows") * height
    pool_kernel = jnp.full((3, 3, filters), 1.0 / 9.0, jnp.float32)
    older_flat = older_output.reshape(-1, channels)
    newer_flat = newer_output.reshape(-1, channels)
    older_relu = jnp.maximum(older_flat, 0)
    newer_relu = jnp.maximum(newer_flat, 0)
    older_full, newer_full = (
        lax.all_gather(older_weight, "rows", axis=0, tiled=True),
        lax.all_gather(newer_weight, "rows", axis=0, tiled=True),
    )
    older_sum = jnp.dot(older_relu, older_full, preferred_element_type=jnp.float32)
    newer_sum = jnp.dot(newer_relu, newer_full, preferred_element_type=jnp.float32)
    older_mixed = older_sum.astype(jnp.bfloat16).reshape(shape_three)
    newer_mixed = newer_sum.astype(jnp.bfloat16).reshape(shape_three)
    square_full, column_full = (
        lax.all_gather(square_point, "rows", axis=0, tiled=True),
        lax.all_gather(column_point, "rows", axis=0, tiled=True),
    )
    older_rim = with_halo(older_mixed, (("rows", 0),), 3)
    newer_rim = with_halo(newer_mixed, (("rows", 0),), 1)
    square_pre = (
        square_taps(newer_rim, square_kernel, False, first_row)
        .astype(jnp.bfloat16)
        .reshape(-1, filters)
    )
    column_pre = (
        column_taps(older_rim, column_kernel, False, first_row)
        .astype(jnp.bfloat16)
        .reshape(-1, filters)
    )
    pooled = square_taps(older_rim[2:-2], pool_kernel, False, first_row).reshape(-1, filters)
    square_branch = jnp.dot(square_pre, square_full, preferred_element_type=jnp.float32)
    column_branch = jnp.dot(column_pre, column_full, preferred_element_type=jnp.float32)
    cell_output = jnp.concatenate(
        [
            square_branch,
            column_branch,
            pooled,
            newer_mixed.reshape(-1, filters).astype(jnp.float32),
        ],
        axis=1,
    )
    cell_output = cell_output.astype(jnp.bfloat16).reshape(height, across, 4 * filters)
    grads = output_grad.reshape(-1, 4 * filters)
    grad_square = grads[:, :filters]
    grad_column = grads[:, filters : 2 * filters]
    grad_pool = grads[:, 2 * filters : 3 * filters].reshape(shape_three)
    grad_same = grads[:, 3 * filters :].reshape(shape_three)
    square_back = (
        jnp.dot(grad_square, square_full.T, preferred_element_type=jnp.float32)
        .astype(jnp.bfloat16)
        .reshape(shape_three)
    )
    column_back = (
        jnp.dot(grad_column, column_full.T, preferred_element_type=jnp.float32)
        .astype(jnp.bfloat16)
        .reshape(shape_three)
    )
    column_rim = with_halo(column_back, (("rows", 0),), 3)
    square_rim, pool_rim = (
        with_halo(square_back, (("rows", 0),), 1),
        with_halo(grad_pool, (("rows", 0),), 1),
    )
    newer_back = (
        (square_taps(square_rim, square_kernel, True, first_row) + grad_same.astype(jnp.float32))
        .astype(jnp.bfloat16)
        .reshape(-1, filters)
    )
    older_back = (
        (
            column_taps(column_rim, column_kernel, True, first_row)
            + square_taps(pool_rim, pool_kernel, True, first_row)
        )
        .astype(jnp.bfloat16)
        .reshape(-1, filters)
    )
    older_mask = jnp.where(older_flat > 0, 1.0, 0.0).astype(jnp.float32)
    newer_mask = jnp.where(newer_flat > 0, 1.0, 0.0).astype(jnp.float32)
    older_term = jnp.dot(older_back, older_full.T, preferred_element_type=jnp.float32)
    newer_term = jnp.dot(newer_back, newer_full.T, preferred_element_type=jnp.float32)
    older_grad = (older_term * older_mask).astype(jnp.bfloat16).reshape(older_output.shape)
    newer_grad = (newer_term * newer_mask).astype(jnp.bfloat16).reshape(newer_output.shape)
    return (cell_output, older_grad, newer_grad)


def solution(mesh):
    in_specs = (
        P(("dp", "rows"), None, None),
        P(("dp", "rows"), None, None),
        P(("dp", "rows"), None, None),
        P("rows", None),
        P("rows", None),
        P("rows", None),
        P("rows", None),
        P(),
        P(),
    )
    out_specs = (
        P(("dp", "rows"), None, None),
        P(("dp", "rows"), None, None),
        P(("dp", "rows"), None, None),
    )
    return jax.shard_map(local, mesh=mesh, in_specs=in_specs, out_specs=out_specs, check_vma=False)
```

profile of v0, /device:TPU:1, one launch (start us, length us, event | category | flops | bytes accessed | tf_op | source)
XLA Modules:
  0.0 140.9 jit_solution(8323920743990531332)
XLA Ops:
  7.2 0.7 all-gather.5.cloned.1.call-update
  8.0 1.6 %copy.52 = bf16[15,12,2048]{2,1,0:T(8,128)(2,1)S(1)} copy(bf16[15,12,2048]{2,0,1:T(8,128)(2,1)} %param.11) | data formatting | bytes 1474560 | tf_op args[2]
  9.7 22.4 %all_gather.13 = bf16[512,512]{1,0:T(8,128)(2,1)S(1)} all-gather(bf16[32,512]{1,0:T(8,128)(2,1)S(1)} %copy-done.40), channel_id=1, replica_groups=mesh['dp'=32,'rows'=16] {'rows'}, dimensions={0}, use_global_device_ids=true | all-gather | bytes 557056 | tf_op jit(solution)/shard_map/all_gather | solution.py:84
  32.1 0.8 copy-done.3
  34.0 3.7 %collective-permute-start.8 = (bf16[1,12,512]{2,1,0:T(8,128)(2,1)}, bf16[1,12,512]{2,1,0:T(8,128)(2,1)}, u32[]{:S(2)}, u32[]{:S(2)}) collective-permute-start(bf16[1,12,512]{2,1,0:T(8,128)(2,1)} %get-tuple-element.18), channel_id=1, source_target_pairs={{0,1},{1,2},{2,3},{3,4},{4,5},{5,6},{6,7},{7,8},{8,9},{9,10},{10,1... | collective-permute-start | bytes 36872 | tf_op jit(solution)/shard_map/ppermute | solution.py:14
  37.7 1.9 %collective-permute-start.9 = (bf16[1,12,512]{2,1,0:T(8,128)(2,1)}, bf16[1,12,512]{2,1,0:T(8,128)(2,1)}, u32[]{:S(2)}, u32[]{:S(2)}) collective-permute-start(bf16[1,12,512]{2,1,0:T(8,128)(2,1)} %get-tuple-element.19), channel_id=1, source_target_pairs={{1,0},{2,1},{3,2},{4,3},{5,4},{6,5},{7,6},{8,7},{9,8},{10,9},{11,1... | collective-permute-start | bytes 36872 | tf_op jit(solution)/shard_map/ppermute | solution.py:17
  40.3 1.9 %collective-permute-start.7 = (bf16[1,12,512]{2,0,1:T(2,128)(2,1)}, bf16[1,12,512]{2,0,1:T(2,128)(2,1)}, u32[]{:S(2)}, u32[]{:S(2)}) collective-permute-start(bf16[1,12,512]{2,0,1:T(2,128)(2,1)} %copy.57), channel_id=1, source_target_pairs={{1,0},{2,1},{3,2},{4,3},{5,4},{6,5},{7,6},{8,7},{9,8},{10,9},{11,1... | collective-permute-start | bytes 36872 | tf_op jit(solution)/shard_map/ppermute | solution.py:17
  42.8 3.6 %collective-permute-start.6 = (bf16[1,12,512]{2,0,1:T(2,128)(2,1)}, bf16[1,12,512]{2,0,1:T(2,128)(2,1)}, u32[]{:S(2)}, u32[]{:S(2)}) collective-permute-start(bf16[1,12,512]{2,0,1:T(2,128)(2,1)} %copy.56), channel_id=1, source_target_pairs={{0,1},{1,2},{2,3},{3,4},{4,5},{5,6},{6,7},{7,8},{8,9},{9,10},{10,1... | collective-permute-start | bytes 36872 | tf_op jit(solution)/shard_map/ppermute | solution.py:14
  46.4 17.1 %all_gather.15 = bf16[512,512]{1,0:T(8,128)(2,1)S(1)} all-gather(bf16[32,512]{1,0:T(8,128)(2,1)S(1)} %copy-done.41), channel_id=1, replica_groups=mesh['dp'=32,'rows'=16] {'rows'}, dimensions={0}, use_global_device_ids=true | all-gather | bytes 557056 | tf_op jit(solution)/shard_map/all_gather | solution.py:85
  63.5 0.8 copy-done.9
  65.9 2.1 %collective-permute-start.5 = (bf16[3,12,512]{2,0,1:T(4,128)(2,1)}, bf16[3,12,512]{2,0,1:T(4,128)(2,1)}, u32[]{:S(2)}, u32[]{:S(2)}) collective-permute-start(bf16[3,12,512]{2,0,1:T(4,128)(2,1)} %copy.54), channel_id=1, source_target_pairs={{1,0},{2,1},{3,2},{4,3},{5,4},{6,5},{7,6},{8,7},{9,8},{10,9},{11,1... | collective-permute-start | bytes 110600 | tf_op jit(solution)/shard_map/ppermute | solution.py:17
  68.2 0.7 broadcast_multiply_fusion.2
  68.9 0.9 broadcast_multiply_fusion.6
  69.8 0.7 broadcast_multiply_fusion.5
  70.5 0.8 slice_convert_fusion
  71.4 0.9 broadcast_maximum_fusion
  72.4 1.3 compare_select_fusion.1
  74.6 0.7 reshape.951
  75.4 0.8 reshape.947
  76.1 1.6 %copy.47 = bf16[15,12,2048]{2,1,0:T(8,128)(2,1)S(1)} copy(bf16[15,12,2048]{2,0,1:T(8,128)(2,1)} %broadcast_maximum_fusion) | data formatting | bytes 1474560 | tf_op jit(solution)/shard_map/max | solution.py:73
  77.7 1.0 max.15
  79.2 1.0 max.13
  80.9 0.8 copy.55
  81.7 0.8 reshape.954
  82.6 0.8 copy.58
  83.4 2.3 %copy.60 = f32[15,12,2048]{2,1,0:T(8,128)S(1)} copy(f32[15,12,2048]{2,0,1:T(8,128)} %compare_select_fusion.1) | data formatting | bytes 2949120 | tf_op jit(solution)/shard_map/jit(_where)/select_n | solution.py:145
  85.7 1.4 select_n.201
  87.0 0.9 copy.61
  88.0 1.3 select_n.203
  89.3 3.5 %collective-permute-start.4 = (bf16[3,12,512]{2,0,1:T(4,128)(2,1)S(1)}, bf16[3,12,512]{2,0,1:T(4,128)(2,1)S(1)}, u32[]{:S(2)}, u32[]{:S(2)}) collective-permute-start(bf16[3,12,512]{2,0,1:T(4,128)(2,1)S(1)} %copy-done.39), channel_id=1, source_target_pairs={{0,1},{1,2},{2,3},{3,4},{4,5},{5,6},{6,7},{7,8},{8,9},{9,10},{10,1... | collective-permute-start | bytes 110600 | tf_op jit(solution)/shard_map/ppermute | solution.py:14
  92.8 0.9 fusion.61
  94.7 0.9 fusion.60
  95.7 0.9 maximum_convert_fusion
  97.4 0.7 reshape.949
  98.1 2.2 %convolution_convert_fusion.4 = bf16[180,512]{1,0:T(8,128)(2,1)S(1)} fusion(bf16[180,2048]{1,0:T(8,128)(2,1)S(1)} %copy-done.8, bf16[2048,512]{1,0:T(8,128)(2,1)} %all-gather.5.cloned.1.call-done), kind=kOutput, calls=%fused_computation.10 | convolution fusion | flops 377579520 | bytes 3018752 | tf_op jit(solution)/shard_map/dot_general | solution.py:79
  100.5 2.1 %collective-permute-start.3 = (bf16[3,12,512]{2,0,1:T(4,128)(2,1)S(1)}, bf16[3,12,512]{2,0,1:T(4,128)(2,1)S(1)}, u32[]{:S(2)}, u32[]{:S(2)}) collective-permute-start(bf16[3,12,512]{2,0,1:T(4,128)(2,1)S(1)} %copy.49), channel_id=1, source_target_pairs={{1,0},{2,1},{3,2},{4,3},{5,4},{6,5},{7,6},{8,7},{9,8},{10,9},{11,1... | collective-permute-start | bytes 110600 | tf_op jit(solution)/shard_map/ppermute | solution.py:17
  102.5 7.8 %all-gather.3.cloned.1.call-done = bf16[2048,512]{1,0:T(8,128)(2,1)} async-done(((bf16[128,512]{1,0:T(8,128)(2,1)}), bf16[2048,512]{1,0:T(8,128)(2,1)}) %all-gather.3.cloned.1.call-update) | async-done | bytes 2097168 | tf_op jit(solution)/shard_map/all_gather | solution.py:77
  110.3 2.1 %convolution_convert_fusion.5 = bf16[180,512]{1,0:T(8,128)(2,1)S(1)} fusion(bf16[180,2048]{1,0:T(8,128)(2,1)S(1)} %copy-done.7, bf16[2048,512]{1,0:T(8,128)(2,1)} %all-gather.3.cloned.1.call-done), kind=kOutput, calls=%fused_computation.11 | convolution fusion | flops 377579520 | bytes 3018752 | tf_op jit(solution)/shard_map/dot_general | solution.py:80
  113.1 2.9 %collective-permute-start = (bf16[1,12,512]{2,1,0:T(8,128)(2,1)}, bf16[1,12,512]{2,1,0:T(8,128)(2,1)}, u32[]{:S(2)}, u32[]{:S(2)}) collective-permute-start(bf16[1,12,512]{2,1,0:T(8,128)(2,1)} %get-tuple-element.22), channel_id=1, source_target_pairs={{0,1},{1,2},{2,3},{3,4},{4,5},{5,6},{6,7},{7,8},{8,9},{9,10},{10,1... | collective-permute-start | bytes 36872 | tf_op jit(solution)/shard_map/ppermute | solution.py:14
  116.0 2.2 %collective-permute-start.1 = (bf16[1,12,512]{2,1,0:T(8,128)(2,1)}, bf16[1,12,512]{2,1,0:T(8,128)(2,1)}, u32[]{:S(2)}, u32[]{:S(2)}) collective-permute-start(bf16[1,12,512]{2,1,0:T(8,128)(2,1)} %get-tuple-element.23), channel_id=1, source_target_pairs={{1,0},{2,1},{3,2},{4,3},{5,4},{6,5},{7,6},{8,7},{9,8},{10,9},{11,1... | collective-permute-start | bytes 36872 | tf_op jit(solution)/shard_map/ppermute | solution.py:17
  118.3 2.3 %fusion = bf16[180,2048]{1,0:T(8,128)(2,1)S(1)} fusion(f32[180,2048]{1,0:T(8,128)} %select_n.201, bf16[180,512]{1,0:T(8,128)(2,1)} %reshape.949, bf16[2048,512]{1,0:T(8,128)(2,1)S(1)} %copy-done), kind=kOutput, calls=%fused_computation.2 | convolution fusion | flops 378224640 | bytes 4493312 | tf_op jit(solution)/shard_map/dot_general | solution.py:147
  120.6 0.8 fusion.1
  121.8 3.8 %collective-permute-start.2 = (bf16[3,12,512]{2,0,1:T(4,128)(2,1)S(1)}, bf16[3,12,512]{2,0,1:T(4,128)(2,1)S(1)}, u32[]{:S(2)}, u32[]{:S(2)}) collective-permute-start(bf16[3,12,512]{2,0,1:T(4,128)(2,1)S(1)} %copy.48), channel_id=1, source_target_pairs={{0,1},{1,2},{2,3},{3,4},{4,5},{5,6},{6,7},{7,8},{8,9},{9,10},{10,1... | collective-permute-start | bytes 110600 | tf_op jit(solution)/shard_map/ppermute | solution.py:14
  125.9 1.3 copy.62
  127.4 1.3 copy.63
  128.7 0.9 fusion.62
  131.9 0.7 copy-done.10
  133.1 1.0 pad_maximum_fusion
  (180 shorter events, 11.9 us)
Async XLA Ops:
  7.2 91.0 %all-gather.5.cloned.1.call-start = ((), (), s32[]{:S(2)}) async-start(), calls=%async_computation.1 | async-start | bytes 2228224 | tf_op jit(solution)/shard_map/all_gather | solution.py:76
  7.9 102.4 %all-gather.3.cloned.1.call-start = ((), (), s32[]{:S(2)}) async-start(), calls=%async_computation | async-start | bytes 2228224 | tf_op jit(solution)/shard_map/all_gather | solution.py:77
  9.5 36.9 %copy-start.41 = (bf16[32,512]{1,0:T(8,128)(2,1)S(1)}, bf16[32,512]{1,0:T(8,128)(2,1)}, u32[]{:S(2)}) copy-start(bf16[32,512]{1,0:T(8,128)(2,1)} %param.15) | copy-start | bytes 98308
  33.0 35.1 %copy-start.55 = (f32[7,512]{1,0:T(8,128)S(1)}, f32[7,512]{1,0:T(8,128)}, u32[]{:S(2)}) copy-start(f32[7,512]{1,0:T(8,128)} %param.17) | copy-start | bytes 43012
  33.0 35.1 %copy-start.54 = (f32[3,3,512]{2,1,0:T(4,128)S(1)}, f32[3,3,512]{2,1,0:T(4,128)}, u32[]{:S(2)}) copy-start(f32[3,3,512]{2,1,0:T(4,128)} %param.16) | copy-start | bytes 55300
  33.3 31.3 %copy-start.15 = (bf16[180,512]{1,0:T(8,128)(2,1)}, bf16[180,512]{1,0:T(8,128)(2,1)S(1)}, u32[]{:S(2)}) copy-start(bf16[180,512]{1,0:T(8,128)(2,1)S(1)} %convolution_convert_fusion.2) | copy-start | bytes 552964
  34.0 55.3 %collective-permute-start.8 = (bf16[1,12,512]{2,1,0:T(8,128)(2,1)}, bf16[1,12,512]{2,1,0:T(8,128)(2,1)}, u32[]{:S(2)}, u32[]{:S(2)}) collective-permute-start(bf16[1,12,512]{2,1,0:T(8,128)(2,1)} %get-tuple-element.18), channel_id=1, source_target_pairs={{0,1},{1,2},{2,3},{3,4},{4,5},{5,6},{6,7},{7,8},{8,9},{9,10},{10,1... | collective-permute-start | bytes 36872 | tf_op jit(solution)/shard_map/ppermute | solution.py:14
  37.7 55.1 %collective-permute-start.9 = (bf16[1,12,512]{2,1,0:T(8,128)(2,1)}, bf16[1,12,512]{2,1,0:T(8,128)(2,1)}, u32[]{:S(2)}, u32[]{:S(2)}) collective-permute-start(bf16[1,12,512]{2,1,0:T(8,128)(2,1)} %get-tuple-element.19), channel_id=1, source_target_pairs={{1,0},{2,1},{3,2},{4,3},{5,4},{6,5},{7,6},{8,7},{9,8},{10,9},{11,1... | collective-permute-start | bytes 36872 | tf_op jit(solution)/shard_map/ppermute | solution.py:17
  40.3 54.0 %collective-permute-start.7 = (bf16[1,12,512]{2,0,1:T(2,128)(2,1)}, bf16[1,12,512]{2,0,1:T(2,128)(2,1)}, u32[]{:S(2)}, u32[]{:S(2)}) collective-permute-start(bf16[1,12,512]{2,0,1:T(2,128)(2,1)} %copy.57), channel_id=1, source_target_pairs={{1,0},{2,1},{3,2},{4,3},{5,4},{6,5},{7,6},{8,7},{9,8},{10,9},{11,1... | collective-permute-start | bytes 36872 | tf_op jit(solution)/shard_map/ppermute | solution.py:17
  42.8 51.5 %collective-permute-start.6 = (bf16[1,12,512]{2,0,1:T(2,128)(2,1)}, bf16[1,12,512]{2,0,1:T(2,128)(2,1)}, u32[]{:S(2)}, u32[]{:S(2)}) collective-permute-start(bf16[1,12,512]{2,0,1:T(2,128)(2,1)} %copy.56), channel_id=1, source_target_pairs={{0,1},{1,2},{2,3},{3,4},{4,5},{5,6},{6,7},{7,8},{8,9},{9,10},{10,1... | collective-permute-start | bytes 36872 | tf_op jit(solution)/shard_map/ppermute | solution.py:14
  64.3 7.1 %copy-start.5 = (bf16[15,12,2048]{2,0,1:T(8,128)(2,1)S(1)}, bf16[15,12,2048]{2,0,1:T(8,128)(2,1)}, u32[]{:S(2)}) copy-start(bf16[15,12,2048]{2,0,1:T(8,128)(2,1)} %param.9) | copy-start | bytes 2211844
  65.9 29.7 %collective-permute-start.5 = (bf16[3,12,512]{2,0,1:T(4,128)(2,1)}, bf16[3,12,512]{2,0,1:T(4,128)(2,1)}, u32[]{:S(2)}, u32[]{:S(2)}) collective-permute-start(bf16[3,12,512]{2,0,1:T(4,128)(2,1)} %copy.54), channel_id=1, source_target_pairs={{1,0},{2,1},{3,2},{4,3},{5,4},{6,5},{7,6},{8,7},{9,8},{10,9},{11,1... | collective-permute-start | bytes 110600 | tf_op jit(solution)/shard_map/ppermute | solution.py:17
  68.1 28.5 %copy-start.56 = (f32[1,512]{1,0:T(1,128)}, f32[1,512]{1,0:T(1,128)S(1)}, u32[]{:S(2)}) copy-start(f32[1,512]{1,0:T(1,128)S(1)} %get-tuple-element.37) | copy-start | bytes 6148
  68.2 25.5 %copy-start.48 = (f32[1,1,512]{2,1,0:T(1,128)}, f32[1,1,512]{2,1,0:T(1,128)S(1)}, u32[]{:S(2)}) copy-start(f32[1,1,512]{2,1,0:T(1,128)S(1)} %get-tuple-element.28) | copy-start | bytes 6148
  68.2 25.5 %copy-start.50 = (f32[1,1,512]{2,1,0:T(1,128)}, f32[1,1,512]{2,1,0:T(1,128)S(1)}, u32[]{:S(2)}) copy-start(f32[1,1,512]{2,1,0:T(1,128)S(1)} %get-tuple-element.29) | copy-start | bytes 6148
  68.2 25.5 %copy-start.52 = (f32[1,1,512]{2,1,0:T(1,128)}, f32[1,1,512]{2,1,0:T(1,128)S(1)}, u32[]{:S(2)}) copy-start(f32[1,1,512]{2,1,0:T(1,128)S(1)} %get-tuple-element.30) | copy-start | bytes 6148
  68.9 3.4 %copy-start.6 = (bf16[15,12,2048]{2,0,1:T(8,128)(2,1)S(1)}, bf16[15,12,2048]{2,0,1:T(8,128)(2,1)}, u32[]{:S(2)}) copy-start(bf16[15,12,2048]{2,0,1:T(8,128)(2,1)} %param.10) | copy-start | bytes 2211844
  79.2 2.5 %copy-start.12 = (f32[180,512]{1,0:T(8,128)S(1)}, f32[180,512]{1,0:T(8,128)}, u32[]{:S(2)}) copy-start(f32[180,512]{1,0:T(8,128)} %get-tuple-element.12) | copy-start | bytes 1105924
  79.2 3.3 %copy-start.19 = (bf16[180,512]{1,0:T(8,128)(2,1)S(1)}, bf16[180,512]{1,0:T(8,128)(2,1)}, u32[]{:S(2)}) copy-start(bf16[180,512]{1,0:T(8,128)(2,1)} %get-tuple-element.13) | copy-start | bytes 552964
  87.9 4.9 %copy-start.14 = (bf16[15,12,512]{2,1,0:T(8,128)(2,1)S(1)}, bf16[15,12,512]{2,1,0:T(8,128)(2,1)}, u32[]{:S(2)}) copy-start(bf16[15,12,512]{2,1,0:T(8,128)(2,1)} %reshape.951) | copy-start | bytes 552964
  87.9 5.8 %copy-start.11 = (f32[15,12,512]{2,1,0:T(8,128)S(1)}, f32[15,12,512]{2,1,0:T(8,128)}, u32[]{:S(2)}) copy-start(f32[15,12,512]{2,1,0:T(8,128)} %reshape.954) | copy-start | bytes 1105924
  87.9 5.8 %copy-start.29 = (f32[15,512]{1,0:T(8,128)S(1)}, f32[15,512]{1,0:T(8,128)}, u32[]{:S(2)}) copy-start(f32[15,512]{1,0:T(8,128)} %get-tuple-element.71) | copy-start | bytes 92164
  88.0 5.8 %copy-start.30 = (f32[15,512]{1,0:T(8,128)S(1)}, f32[15,512]{1,0:T(8,128)}, u32[]{:S(2)}) copy-start(f32[15,512]{1,0:T(8,128)} %get-tuple-element.73) | copy-start | bytes 92164
  88.0 5.8 %copy-start.31 = (f32[15,512]{1,0:T(8,128)S(1)}, f32[15,512]{1,0:T(8,128)}, u32[]{:S(2)}) copy-start(f32[15,512]{1,0:T(8,128)} %get-tuple-element.75) | copy-start | bytes 92164
  88.0 5.8 %copy-start.32 = (f32[15,512]{1,0:T(8,128)S(1)}, f32[15,512]{1,0:T(8,128)}, u32[]{:S(2)}) copy-start(f32[15,512]{1,0:T(8,128)} %get-tuple-element.77) | copy-start | bytes 92164
  88.0 5.8 %copy-start.33 = (f32[15,512]{1,0:T(8,128)S(1)}, f32[15,512]{1,0:T(8,128)}, u32[]{:S(2)}) copy-start(f32[15,512]{1,0:T(8,128)} %get-tuple-element.79) | copy-start | bytes 92164
  88.0 5.8 %copy-start.34 = (f32[15,512]{1,0:T(8,128)S(1)}, f32[15,512]{1,0:T(8,128)}, u32[]{:S(2)}) copy-start(f32[15,512]{1,0:T(8,128)} %get-tuple-element.81) | copy-start | bytes 92164
  89.3 6.3 %collective-permute-start.4 = (bf16[3,12,512]{2,0,1:T(4,128)(2,1)S(1)}, bf16[3,12,512]{2,0,1:T(4,128)(2,1)S(1)}, u32[]{:S(2)}, u32[]{:S(2)}) collective-permute-start(bf16[3,12,512]{2,0,1:T(4,128)(2,1)S(1)} %copy-done.39), channel_id=1, source_target_pairs={{0,1},{1,2},{2,3},{3,4},{4,5},{5,6},{6,7},{7,8},{8,9},{9,10},{10,1... | collective-permute-start | bytes 110600 | tf_op jit(solution)/shard_map/ppermute | solution.py:14
  94.2 2.4 %copy-start.27 = (f32[15,512]{1,0:T(8,128)S(1)}, f32[15,512]{1,0:T(8,128)}, u32[]{:S(2)}) copy-start(f32[15,512]{1,0:T(8,128)} %get-tuple-element.60) | copy-start | bytes 92164
  94.2 2.4 %copy-start.28 = (f32[15,512]{1,0:T(8,128)S(1)}, f32[15,512]{1,0:T(8,128)}, u32[]{:S(2)}) copy-start(f32[15,512]{1,0:T(8,128)} %get-tuple-element.83) | copy-start | bytes 92164
  94.2 2.4 %copy-start.35 = (f32[15,512]{1,0:T(8,128)S(1)}, f32[15,512]{1,0:T(8,128)}, u32[]{:S(2)}) copy-start(f32[15,512]{1,0:T(8,128)} %get-tuple-element.64) | copy-start | bytes 92164
  94.3 2.4 %copy-start.36 = (f32[15,512]{1,0:T(8,128)S(1)}, f32[15,512]{1,0:T(8,128)}, u32[]{:S(2)}) copy-start(f32[15,512]{1,0:T(8,128)} %get-tuple-element.67) | copy-start | bytes 92164
  94.3 2.4 %copy-start.37 = (f32[15,512]{1,0:T(8,128)S(1)}, f32[15,512]{1,0:T(8,128)}, u32[]{:S(2)}) copy-start(f32[15,512]{1,0:T(8,128)} %get-tuple-element.62) | copy-start | bytes 92164
  94.3 2.4 %copy-start.38 = (f32[15,512]{1,0:T(8,128)S(1)}, f32[15,512]{1,0:T(8,128)}, u32[]{:S(2)}) copy-start(f32[15,512]{1,0:T(8,128)} %get-tuple-element.69) | copy-start | bytes 92164
  94.3 2.4 %copy-start.58 = (f32[15]{0:T(128)S(1)}, f32[15]{0:T(128)}, u32[]{:S(2)}) copy-start(f32[15]{0:T(128)} %get-tuple-element.90) | copy-start | bytes 184
  94.3 2.4 %copy-start.60 = (f32[15]{0:T(128)S(1)}, f32[15]{0:T(128)}, u32[]{:S(2)}) copy-start(f32[15]{0:T(128)} %get-tuple-element.91) | copy-start | bytes 184
  98.1 12.2 %copy-start.7 = (bf16[180,2048]{1,0:T(8,128)(2,1)S(1)}, bf16[180,2048]{1,0:T(8,128)(2,1)}, u32[]{:S(2)}) copy-start(bf16[180,2048]{1,0:T(8,128)(2,1)} %max.13) | copy-start | bytes 2211844
  100.5 17.8 %copy-start = (bf16[2048,512]{1,0:T(8,128)(2,1)S(1)}, bf16[2048,512]{1,0:T(8,128)(2,1)}, u32[]{:S(2)}) copy-start(bf16[2048,512]{1,0:T(8,128)(2,1)} %all-gather.5.cloned.1.call-done) | copy-start | bytes 6291460
  100.5 30.5 %collective-permute-start.3 = (bf16[3,12,512]{2,0,1:T(4,128)(2,1)S(1)}, bf16[3,12,512]{2,0,1:T(4,128)(2,1)S(1)}, u32[]{:S(2)}, u32[]{:S(2)}) collective-permute-start(bf16[3,12,512]{2,0,1:T(4,128)(2,1)S(1)} %copy.49), channel_id=1, source_target_pairs={{1,0},{2,1},{3,2},{4,3},{5,4},{6,5},{7,6},{8,7},{9,8},{10,9},{11,1... | collective-permute-start | bytes 110600 | tf_op jit(solution)/shard_map/ppermute | solution.py:17
  113.1 15.6 %collective-permute-start = (bf16[1,12,512]{2,1,0:T(8,128)(2,1)}, bf16[1,12,512]{2,1,0:T(8,128)(2,1)}, u32[]{:S(2)}, u32[]{:S(2)}) collective-permute-start(bf16[1,12,512]{2,1,0:T(8,128)(2,1)} %get-tuple-element.22), channel_id=1, source_target_pairs={{0,1},{1,2},{2,3},{3,4},{4,5},{5,6},{6,7},{7,8},{8,9},{9,10},{10,1... | collective-permute-start | bytes 36872 | tf_op jit(solution)/shard_map/ppermute | solution.py:14
  116.0 4.6 %copy-start.1 = (bf16[2048,512]{1,0:T(8,128)(2,1)S(1)}, bf16[2048,512]{1,0:T(8,128)(2,1)}, u32[]{:S(2)}) copy-start(bf16[2048,512]{1,0:T(8,128)(2,1)} %all-gather.3.cloned.1.call-done) | copy-start | bytes 6291460
  116.0 4.6 %copy-start.2 = (f32[180,2048]{1,0:T(8,128)S(1)}, f32[180,2048]{1,0:T(8,128)}, u32[]{:S(2)}) copy-start(f32[180,2048]{1,0:T(8,128)} %select_n.203) | copy-start | bytes 4423684
  116.0 12.6 %collective-permute-start.1 = (bf16[1,12,512]{2,1,0:T(8,128)(2,1)}, bf16[1,12,512]{2,1,0:T(8,128)(2,1)}, u32[]{:S(2)}, u32[]{:S(2)}) collective-permute-start(bf16[1,12,512]{2,1,0:T(8,128)(2,1)} %get-tuple-element.23), channel_id=1, source_target_pairs={{1,0},{2,1},{3,2},{4,3},{5,4},{6,5},{7,6},{8,7},{9,8},{10,9},{11,1... | collective-permute-start | bytes 36872 | tf_op jit(solution)/shard_map/ppermute | solution.py:17
  121.8 9.2 %collective-permute-start.2 = (bf16[3,12,512]{2,0,1:T(4,128)(2,1)S(1)}, bf16[3,12,512]{2,0,1:T(4,128)(2,1)S(1)}, u32[]{:S(2)}, u32[]{:S(2)}) collective-permute-start(bf16[3,12,512]{2,0,1:T(4,128)(2,1)S(1)} %copy.48), channel_id=1, source_target_pairs={{0,1},{1,2},{2,3},{3,4},{4,5},{5,6},{6,7},{7,8},{8,9},{9,10},{10,1... | collective-permute-start | bytes 110600 | tf_op jit(solution)/shard_map/ppermute | solution.py:14
  127.3 2.2 %copy-start.21 = (f32[15,512]{1,0:T(8,128)S(1)}, f32[15,512]{1,0:T(8,128)}, u32[]{:S(2)}) copy-start(f32[15,512]{1,0:T(8,128)} %get-tuple-element.70) | copy-start | bytes 92164
  127.3 2.2 %copy-start.22 = (f32[15,512]{1,0:T(8,128)S(1)}, f32[15,512]{1,0:T(8,128)}, u32[]{:S(2)}) copy-start(f32[15,512]{1,0:T(8,128)} %get-tuple-element.72) | copy-start | bytes 92164
  127.3 2.2 %copy-start.23 = (f32[15,512]{1,0:T(8,128)S(1)}, f32[15,512]{1,0:T(8,128)}, u32[]{:S(2)}) copy-start(f32[15,512]{1,0:T(8,128)} %get-tuple-element.74) | copy-start | bytes 92164
  127.3 2.2 %copy-start.24 = (f32[15,512]{1,0:T(8,128)S(1)}, f32[15,512]{1,0:T(8,128)}, u32[]{:S(2)}) copy-start(f32[15,512]{1,0:T(8,128)} %get-tuple-element.76) | copy-start | bytes 92164
  (26 other events, 35.1 us)
Sparse Core Ops, SparseCore 0:
  10.1 47.4 all-gather.4
  68.1 42.1 all-gather.2
where the time goes:
time: 142 us; the launch traced here: 141 us
  blocking collectives  39.5 us (28%)
  local copies, waits for them, and re-layouts  28.5 us (20%)
  starting transfers between devices  27.8 us (20%)
  between operations  15.2 us (11%)
  other arithmetic  12.5 us (9%)
  matrix products  8.93 us (6%)
  waiting for transfers between devices  8.54 us (6%)
    all_gather x1, blocking collectives, local(): lax.all_gather(square_point, 'rows', axis=0, tiled=True)  22.4 us
    ppermute x5, starting transfers between devices, with_halo(): lax.ppermute(lax.slice_in_dim(block, block.shape[dim] - width, None, axis...  17.5 us
    all_gather x1, blocking collectives, local(): lax.all_gather(column_point, 'rows', axis=0, tiled=True)  17.1 us
    ppermute x5, starting transfers between devices, with_halo(): lax.ppermute(lax.slice_in_dim(block, 0, width, axis=dim), axis, backward)  10.2 us
    unnamed x127, local copies, waits for them, and re-layouts  8.35 us
    all_gather x1, waiting for transfers between devices, local(): lax.all_gather(newer_weight, 'rows', axis=0, tiled=True)  7.82 us
    select_n x2, local copies, waits for them, and re-layouts, local(): older_mask = jnp.where(older_flat > 0, 1.0, 0.0).astype(jnp.float32)  3.64 us
    slice x10, local copies, waits for them, and re-layouts, with_halo(): lax.slice_in_dim(block, block.shape[dim] - width, None, axis=dim)  3.23 us
  transfers between devices with their start and end apart: 12, of which 1 were waited for; matrix products, arithmetic and copies ran while one was open for 31% of the time, Pallas kernels for 0%

commit v1 on v0

v1 whole, which is shorter than its diff:
```python
import jax
import jax.numpy as jnp
from jax import lax
from jax.experimental import pallas as pl
from jax.experimental.pallas import tpu as pltpu
from jax.sharding import PartitionSpec as P

F32 = jnp.float32
BF16 = jnp.bfloat16
C = 512
CIN = 2048
WIDE = 12
ROWS = 15
LANES = 128
BLOCKS = C // LANES
PIECES = 4
SCALE = 2.0**17


def dot(a, b):
    return jnp.dot(a, b, preferred_element_type=F32)


def dot_t(a, b):
    return lax.dot_general(a, b, (((1,), (1,)), ((), ())), preferred_element_type=F32)


def halo_kernel(
    core_ref, xo_hbm, xn_hbm, g_hbm, wo_hbm, wn_hbm, ps_hbm, pc_hbm,
    xo_out, xn_out, g_out, h_out, w_out,
    raw, sems, weight_sems,
):
    first = core_ref[0] == 0
    turn = jnp.where(first, 1, 7)
    fields = ((xo_hbm, xo_out, True), (xn_hbm, xn_out, True), (g_hbm, g_out, False))
    copies = []
    for at, (src, _, _) in enumerate(fields):
        for q in range(PIECES):
            part = pl.ds(q * (WIDE // PIECES), WIDE // PIECES)
            copy = pltpu.make_async_copy(src.at[part], raw.at[at, part], sems.at[at, q])
            copy.start()
            copies.append(copy)
    row = 0
    loads = []
    for at, src in enumerate((wo_hbm, wn_hbm, ps_hbm, pc_hbm)):
        size = src.shape[0]
        copy = pltpu.make_async_copy(src, w_out.at[pl.ds(row, size)], weight_sems.at[at])
        copy.start()
        loads.append(copy)
        row += size
    for at, (_, dst, relu) in enumerate(fields):
        dst[:, 8:16, :] = jnp.zeros((WIDE, 8, CIN), BF16)
        for q in range(PIECES):
            copies[at * PIECES + q].wait()
        v = raw[at]
        dst[:, 0:ROWS, :] = jnp.maximum(v, 0) if relu else v
        sent = jnp.where(first, dst[:, 8:16, :].astype(F32), dst[:, 0:8, :].astype(F32))
        h_out[:, :, at * CIN : (at + 1) * CIN] = pltpu.roll(sent, turn, 1).astype(BF16)
    for copy in loads:
        copy.wait()


def cell_kernel(
    core_ref, xo_s, xn_s, g_s, h_ref, wo_ref, wn_ref, ps_ref, pc_ref, ks_ref, kc_ref,
    cell_hbm, og_hbm, ng_hbm,
    zo, zn, zs, zc, zp, cell_s, og_s, ng_s, sems,
):
    slot = lax.broadcasted_iota(jnp.int32, (1, 8, LANES), 1)
    first = core_ref[0] == 0
    above = jnp.where((slot >= 5) & jnp.logical_not(first), 1.0, 0.0).astype(F32)
    below = jnp.where((slot < 2) & first, 1.0, 0.0).astype(F32)
    edge = jnp.where((slot == 7) & first, 1.0, 0.0).astype(F32)

    for z in (zo, zn, zs, zp):
        z[:, 0] = jnp.zeros((BLOCKS, 32, LANES), F32)
        z[:, WIDE + 1] = jnp.zeros((BLOCKS, 32, LANES), F32)

    def fill(z, own, halo):
        own = own.astype(BF16).astype(F32).reshape(WIDE, 16, C)
        halo = halo.astype(BF16).astype(F32).reshape(WIDE, 8, C)
        for b in range(BLOCKS):
            o = own[:, :, b * LANES : (b + 1) * LANES]
            h = halo[:, :, b * LANES : (b + 1) * LANES]
            z[b, 1 : WIDE + 1, 0:8, :] = h * above
            z[b, 1 : WIDE + 1, 8:16, :] = o[:, 0:8]
            z[b, 1 : WIDE + 1, 16:24, :] = o[:, 8:16] + h * edge
            z[b, 1 : WIDE + 1, 24:32, :] = h * below

    def column(z, b, flip):
        acc = None
        for i in range(7):
            at = 5 + (6 - i if flip else i)
            k = kc_ref[i : i + 1, b * LANES : (b + 1) * LANES].reshape(1, 1, LANES)
            t = z[b, 1 : WIDE + 1, at : at + 16, :] * k
            acc = t if acc is None else acc + t
        return acc

    def square(z, b, flip):
        acc = None
        for i in range(3):
            at = 7 + (2 - i if flip else i)
            for j in range(3):
                w = 2 - j if flip else j
                k = ks_ref[i, j : j + 1, b * LANES : (b + 1) * LANES].reshape(1, 1, LANES)
                t = z[b, w : w + WIDE, at : at + 16, :] * k
                acc = t if acc is None else acc + t
        return acc

    def pool(z, b):
        rows = (
            z[b, :, 7 : 7 + 16, :] + z[b, :, 8 : 8 + 16, :] + z[b, :, 9 : 9 + 16, :]
        )
        return (rows[0:WIDE] + rows[1 : WIDE + 1] + rows[2 : WIDE + 2]) * (1.0 / 9.0)

    def gather(parts):
        return jnp.concatenate([p.astype(BF16).reshape(WIDE * 16, LANES) for p in parts], axis=1)

    copies = []

    def put(stage, hbm, j, value):
        stage[j] = value.astype(BF16).reshape(WIDE, 16, C)[:, 0:ROWS, :]
        copy = pltpu.make_async_copy(
            stage.at[j], hbm.at[:, :, pl.ds(j * C, C)], sems.at[len(copies)]
        )
        copy.start()
        copies.append(copy)

    def flat(ref, lo, hi):
        v = ref[:, :, lo:hi]
        return v.reshape(-1, hi - lo)

    ps = ps_ref[...]
    pc = pc_ref[...]
    fill(zs, dot_t(flat(g_s, 0, C), ps), dot_t(flat(h_ref, 2 * CIN, 2 * CIN + C), ps))
    fill(
        zc,
        dot_t(flat(g_s, C, 2 * C), pc),
        dot_t(flat(h_ref, 2 * CIN + C, 2 * CIN + 2 * C), pc),
    )
    fill(zp, flat(g_s, 2 * C, 3 * C), flat(h_ref, 2 * CIN + 2 * C, 2 * CIN + 3 * C))
    wo = wo_ref[...]
    wn = wn_ref[...]
    fill(zo, dot(flat(xo_s, 0, CIN), wo), dot(flat(h_ref, 0, CIN), wo))
    mixed = dot(flat(xn_s, 0, CIN), wn)
    fill(zn, mixed, dot(flat(h_ref, CIN, 2 * CIN), wn))
    put(cell_s, cell_hbm, 3, mixed)

    back = gather(
        [
            square(zs, b, True)
            + g_s[:, :, 3 * C + b * LANES : 3 * C + (b + 1) * LANES].astype(F32)
            for b in range(BLOCKS)
        ]
    )
    for j in range(4):
        term = dot_t(back, wn_ref[j * C : (j + 1) * C, :])
        put(ng_s, ng_hbm, j, jnp.where(flat(xn_s, j * C, (j + 1) * C).astype(F32) > 0, term, 0.0))
    back = gather([column(zc, b, True) + pool(zp, b) for b in range(BLOCKS)])
    for j in range(4):
        term = dot_t(back, wo_ref[j * C : (j + 1) * C, :])
        put(og_s, og_hbm, j, jnp.where(flat(xo_s, j * C, (j + 1) * C).astype(F32) > 0, term, 0.0))
    put(cell_s, cell_hbm, 0, dot(gather([square(zn, b, False) for b in range(BLOCKS)]), ps))
    put(cell_s, cell_hbm, 1, dot(gather([column(zo, b, False) for b in range(BLOCKS)]), pc))
    put(cell_s, cell_hbm, 2, gather([pool(zo, b) for b in range(BLOCKS)]))
    for copy in copies:
        copy.wait()


def placed(values, space):
    return [pltpu.with_memory_space_constraint(v, space) for v in values]


def run_halo(core, *operands):
    vmem = pl.BlockSpec(memory_space=pltpu.VMEM)
    hbm = pl.BlockSpec(memory_space=pltpu.HBM)
    padded = pltpu.VMEM((WIDE, 16, CIN), BF16)
    shards = sum(v.shape[0] for v in operands[3:])
    return pl.pallas_call(
        halo_kernel,
        out_shape=(padded,) * 3
        + (pltpu.VMEM((WIDE, 8, 3 * CIN), BF16), pltpu.VMEM((shards, C), BF16)),
        in_specs=[pl.BlockSpec(memory_space=pltpu.SMEM)] + [hbm] * 7,
        out_specs=(vmem,) * 5,
        scratch_shapes=[
            pltpu.VMEM((3, WIDE, ROWS, CIN), BF16),
            pltpu.SemaphoreType.DMA((3, PIECES)),
            pltpu.SemaphoreType.DMA((4,)),
        ],
        compiler_params=pltpu.CompilerParams(vmem_limit_bytes=16 * 1024 * 1024),
        name="halo",
    )(core, *placed(operands, pltpu.HBM))


def run_cell(core, *operands):
    vmem = pl.BlockSpec(memory_space=pltpu.VMEM)
    out = jax.ShapeDtypeStruct((WIDE, ROWS, CIN), BF16)
    field = pltpu.VMEM((BLOCKS, WIDE + 2, 32, LANES), F32)
    stage = pltpu.VMEM((4, WIDE, ROWS, C), BF16)
    return pl.pallas_call(
        cell_kernel,
        out_shape=(out, out, out),
        in_specs=[pl.BlockSpec(memory_space=pltpu.SMEM)] + [vmem] * 10,
        out_specs=(pl.BlockSpec(memory_space=pl.ANY),) * 3,
        scratch_shapes=[field] * 5 + [stage] * 3 + [pltpu.SemaphoreType.DMA((12,))],
        compiler_params=pltpu.CompilerParams(vmem_limit_bytes=24 * 1024 * 1024),
        name="cell",
    )(core, *placed(operands, pltpu.VMEM))


def local(
    older_output,
    newer_output,
    output_grad,
    older_weight,
    newer_weight,
    square_point,
    column_point,
    square_kernel,
    column_kernel,
):
    count = lax.axis_size("rows")
    core = lax.rem(lax.axis_index("rows"), 2)
    core = core.astype(jnp.int32).reshape(1)
    xo, xn, grad, rim, shard = run_halo(
        core,
        older_output.transpose(1, 0, 2),
        newer_output.transpose(1, 0, 2),
        output_grad.transpose(1, 0, 2),
        older_weight,
        newer_weight,
        square_point,
        column_point,
    )
    rim = lax.ppermute(rim, "rows", [(i, i ^ 1) for i in range(count)])
    shard = (shard * jnp.asarray(SCALE, BF16)).astype(jnp.float16)
    full = lax.all_gather(shard, "rows", axis=0, tiled=False)

    def part(lo, hi):
        piece = (full[:, lo:hi].astype(F32) * (1.0 / SCALE)).astype(BF16)
        return piece.reshape(-1, C)

    k = older_weight.shape[0]
    p = square_point.shape[0]
    cell, og, ng = run_cell(
        core,
        xo,
        xn,
        grad,
        rim,
        part(0, k),
        part(k, 2 * k),
        part(2 * k, 2 * k + p),
        part(2 * k + p, 2 * k + 2 * p),
        square_kernel,
        column_kernel,
    )
    return cell.transpose(1, 0, 2), og.transpose(1, 0, 2), ng.transpose(1, 0, 2)


def solution(mesh):
    rows = P(("dp", "rows"), None, None)
    in_specs = (rows, rows, rows) + (P("rows", None),) * 4 + (P(), P())
    return jax.shard_map(
        local, mesh=mesh, in_specs=in_specs, out_specs=(rows,) * 3, check_vma=False
    )
```

time: 142 us -> 56.9 us (0.40)
  local copies, waits for them, and re-layouts: 28.5 us -> 0.01 us
  starting transfers between devices: 27.8 us -> 8.75 us
  between operations: 15.2 us -> 0.71 us
  other arithmetic: 12.5 us -> 1.56 us
  matrix products: 8.93 us -> 0 us
  waiting for transfers between devices: 8.54 us -> 0.01 us
  Pallas kernels: 0 us -> 7.86 us
  blocking collectives: 39.5 us -> 37.8 us
    ppermute x10 -> x1, starting transfers between devices: 27.7 us -> 8.75 us  [local(): rim = lax.ppermute(rim, 'rows', [(i, i ^ 1) for i in range(count)])]
    dot_general x8 -> x0, matrix products: 8.93 us -> none  [the longest x1 2.33 us: local(): jnp.dot(older_back, older_full.T, preferred_element_type=jnp.float32)]
    unnamed x127 -> x4, local copies, waits for them, and re-layouts: 8.35 us -> 0.01 us
    pallas_call x0 -> x2, Pallas kernels: none -> 7.86 us  [the longest x1 5.7 us: run_cell(): pl.pallas_call(cell_kernel, out_shape=(out, out, out), in_specs=[pl.Block...]
    all_gather x2 -> x0, waiting for transfers between devices: 7.82 us -> none  [the longest x1 7.82 us: local(): lax.all_gather(newer_weight, 'rows', axis=0, tiled=True)]
    select_n x4 -> x0, local copies, waits for them, and re-layouts: 5.84 us -> none  [the longest x2 3.64 us: local(): older_mask = jnp.where(older_flat > 0, 1.0, 0.0).astype(jnp.float32)]
    reshape x14 -> x0, local copies, waits for them, and re-layouts: 4.65 us -> none  [the longest x2 1.53 us: local(): column_back = jnp.dot(grad_column, column_full.T, preferred_element_type=...]
    slice x18 -> x0, local copies, waits for them, and re-layouts: 4.65 us -> none  [the longest x10 3.23 us: with_halo(): lax.slice_in_dim(block, block.shape[dim] - width, None, axis=dim)]
  transfers between devices with their start and end apart: 12 -> 1, of which waited for: 1 -> 0; matrix products, arithmetic and copies ran while one was open for 31% -> 3% of each run, Pallas kernels for 0% -> 0%
where the time goes in v1:
time: 56.9 us; the launch traced here: 56.7 us
  blocking collectives  37.8 us (66%)
  starting transfers between devices  8.75 us (15%)
  Pallas kernels  7.86 us (14%)
  other arithmetic  1.56 us (3%)
  between operations  0.71 us (1%)
    all_gather x1, blocking collectives, local(): full = lax.all_gather(shard, 'rows', axis=0, tiled=False)  37.8 us
    ppermute x1, starting transfers between devices, local(): rim = lax.ppermute(rim, 'rows', [(i, i ^ 1) for i in range(count)])  8.75 us
    pallas_call x1, Pallas kernels, run_cell(): pl.pallas_call(cell_kernel, out_shape=(out, out, out), in_specs=[pl.Block...  5.7 us
    pallas_call x1, Pallas kernels, run_halo(): pl.pallas_call(halo_kernel, out_shape=(padded,) * 3 + (pltpu.VMEM((WIDE,...  2.16 us
    convert_element_type x2, other arithmetic, part(): piece = (full[:, lo:hi].astype(F32) * (1.0 / SCALE)).astype(BF16)  1.49 us
  transfers between devices with their start and end apart: 1, of which 0 were waited for; matrix products, arithmetic and copies ran while one was open for 3% of the time, Pallas kernels for 0%

profile of v1, /device:TPU:1, one launch (start us, length us, event | category | flops | bytes accessed | tf_op | source)
XLA Modules:
  0.0 56.7 jit_solution(669219842146145980)
XLA Ops:
  0.6 2.2 %halo.1 = (bf16[12,16,2048]{2,1,0:T(8,128)(2,1)S(1)}, bf16[12,16,2048]{2,1,0:T(8,128)(2,1)S(1)}, bf16[12,16,2048]{2,1,0:T(8,128)(2,1)S(1)}, bf16[12,8,6144]{2,1,0:T(8,128)(2,1)S(1)}, bf16[320,512]{1,0:T(8,128)(2,1)S(1)}) custom-call(s32[1]{0:T(128)} %bitcast.core_ref, bf16[12,15,2048]{2,1,0:T(8,128)(2,1)} %bitcast.18, bf16[12,15,2048]{2,1,0:T(8,128)(2,1)} %bitcast.19, ...), custom_call_target="tpu_custom_call" | custom-call | tf_op jit(solution)/shard_map/halo/pallas_call | solution.py:178
  2.8 8.7 %collective-permute-start = (bf16[12,8,6144]{2,1,0:T(8,128)(2,1)S(1)}, bf16[12,8,6144]{2,1,0:T(8,128)(2,1)S(1)}, u32[]{:S(2)}, u32[]{:S(2)}) collective-permute-start(bf16[12,8,6144]{2,1,0:T(8,128)(2,1)S(1)} %get-tuple-element.14), channel_id=1, source_target_pairs={{0,1},{1,0},{2,3},{3,2},{4,5},{5,4},{6,7},{7,6},{8,9},{9,8},{10,11... | collective-permute-start | bytes 3538952 | tf_op jit(solution)/shard_map/ppermute | solution.py:234
  11.6 0.1 multiply_convert_fusion.4
  11.6 37.8 %all-gather.2 = f16[5120,512]{1,0:T(8,128)(2,1)S(1)} all-gather(f16[320,512]{1,0:T(8,128)(2,1)S(1)} %multiply_convert_fusion.4), channel_id=2, replica_groups=mesh['dp'=32,'rows'=16] {'rows'}, dimensions={0}, use_global_device_ids=true | all-gather | bytes 5570560 | tf_op jit(solution)/shard_map/all_gather | solution.py:236
  49.4 0.2 multiply_convert_fusion.2
  49.7 0.0 copy-start
  49.7 0.0 copy-start.1
  49.7 1.2 %multiply_convert_fusion = (bf16[16,128,512]{2,1,0:T(8,128)(2,1)S(1)}, bf16[16,128,512]{2,1,0:T(8,128)(2,1)S(1)}) fusion(f16[16,320,512]{2,1,0:T(8,128)(2,1)S(1)} %bitcast.17), kind=kLoop, calls=%fused_computation | loop fusion | flops 6291456 | bytes 8388608 | tf_op jit(solution)/shard_map/convert_element_type | solution.py:239
  51.0 0.0 collective-permute-done.h_ref
  51.0 0.0 copy-done
  51.0 0.0 copy-done.1
  51.0 5.7 %cell.1 = (bf16[12,15,2048]{2,1,0:T(8,128)(2,1)}, bf16[12,15,2048]{2,1,0:T(8,128)(2,1)}, bf16[12,15,2048]{2,1,0:T(8,128)(2,1)}) custom-call(s32[1]{0:T(128)} %bitcast.core_ref, bf16[12,16,2048]{2,1,0:T(8,128)(2,1)S(1)} %get-tuple-element.11.xo_s, bf16[12,16,2048]{2,1,0:T(8,128)(2,1)S(1)} %get-tuple-element.12.xn_s, ...), custom_call_target="tpu_custom_call" | custom-call | tf_op jit(solution)/shard_map/cell/pallas_call | solution.py:199
Async XLA Ops:
  2.8 48.2 %collective-permute-start = (bf16[12,8,6144]{2,1,0:T(8,128)(2,1)S(1)}, bf16[12,8,6144]{2,1,0:T(8,128)(2,1)S(1)}, u32[]{:S(2)}, u32[]{:S(2)}) collective-permute-start(bf16[12,8,6144]{2,1,0:T(8,128)(2,1)S(1)} %get-tuple-element.14), channel_id=1, source_target_pairs={{0,1},{1,0},{2,3},{3,2},{4,5},{5,4},{6,7},{7,6},{8,9},{9,8},{10,11... | collective-permute-start | bytes 3538952 | tf_op jit(solution)/shard_map/ppermute | solution.py:234
  49.7 1.3 %copy-start = (f32[3,3,512]{2,1,0:T(4,128)S(1)}, f32[3,3,512]{2,1,0:T(4,128)}, u32[]{:S(2)}) copy-start(f32[3,3,512]{2,1,0:T(4,128)} %ks_ref.1) | copy-start | bytes 55300
  49.7 1.3 %copy-start.1 = (f32[7,512]{1,0:T(8,128)S(1)}, f32[7,512]{1,0:T(8,128)}, u32[]{:S(2)}) copy-start(f32[7,512]{1,0:T(8,128)} %kc_ref.1) | copy-start | bytes 43012

commit v2 on v1

--- a/solution.py
+++ b/solution.py
@@ -15,6 +15,7 @@
 BLOCKS = C // LANES
 PIECES = 4
 SCALE = 2.0**17
+UNSCALE = 1.0 / SCALE
 
 
 def dot(a, b):
@@ -76,9 +77,9 @@
         z[:, WIDE + 1] = jnp.zeros((BLOCKS, 32, LANES), F32)
 
     def fill(z, own, halo):
-        own = own.astype(BF16).astype(F32).reshape(WIDE, 16, C)
-        halo = halo.astype(BF16).astype(F32).reshape(WIDE, 8, C)
-        for b in range(BLOCKS):
+        own = own.astype(BF16).astype(F32).reshape(WIDE, 16, -1)
+        halo = halo.astype(BF16).astype(F32).reshape(WIDE, 8, -1)
+        for b in range(own.shape[2] // LANES):
             o = own[:, :, b * LANES : (b + 1) * LANES]
             h = halo[:, :, b * LANES : (b + 1) * LANES]
             z[b, 1 : WIDE + 1, 0:8, :] = h * above
@@ -86,22 +87,27 @@
             z[b, 1 : WIDE + 1, 16:24, :] = o[:, 8:16] + h * edge
             z[b, 1 : WIDE + 1, 24:32, :] = h * below
 
-    def column(z, b, flip):
+    def fill_all(z, both):
+        fill(z, both[: WIDE * 16], both[WIDE * 16 :])
+
+    def column(z, b, flip, scale=None):
         acc = None
         for i in range(7):
             at = 5 + (6 - i if flip else i)
             k = kc_ref[i : i + 1, b * LANES : (b + 1) * LANES].reshape(1, 1, LANES)
+            k = k if scale is None else k * scale
             t = z[b, 1 : WIDE + 1, at : at + 16, :] * k
             acc = t if acc is None else acc + t
         return acc
 
-    def square(z, b, flip):
+    def square(z, b, flip, scale=None):
         acc = None
         for i in range(3):
             at = 7 + (2 - i if flip else i)
             for j in range(3):
                 w = 2 - j if flip else j
                 k = ks_ref[i, j : j + 1, b * LANES : (b + 1) * LANES].reshape(1, 1, LANES)
+                k = k if scale is None else k * scale
                 t = z[b, w : w + WIDE, at : at + 16, :] * k
                 acc = t if acc is None else acc + t
         return acc
@@ -129,39 +135,55 @@
         v = ref[:, :, lo:hi]
         return v.reshape(-1, hi - lo)
 
+    def rows_of(ref, lo, hi, halo_lo):
+        return jnp.concatenate([flat(ref, lo, hi), flat(h_ref, halo_lo, halo_lo + hi - lo)], axis=0)
+
     ps = ps_ref[...]
     pc = pc_ref[...]
-    fill(zs, dot_t(flat(g_s, 0, C), ps), dot_t(flat(h_ref, 2 * CIN, 2 * CIN + C), ps))
-    fill(
-        zc,
-        dot_t(flat(g_s, C, 2 * C), pc),
-        dot_t(flat(h_ref, 2 * CIN + C, 2 * CIN + 2 * C), pc),
-    )
+    fill_all(zs, dot_t(rows_of(g_s, 0, C, 2 * CIN), ps) * UNSCALE)
+    fill_all(zc, dot_t(rows_of(g_s, C, 2 * C, 2 * CIN + C), pc) * UNSCALE)
     fill(zp, flat(g_s, 2 * C, 3 * C), flat(h_ref, 2 * CIN + 2 * C, 2 * CIN + 3 * C))
-    wo = wo_ref[...]
-    wn = wn_ref[...]
-    fill(zo, dot(flat(xo_s, 0, CIN), wo), dot(flat(h_ref, 0, CIN), wo))
-    mixed = dot(flat(xn_s, 0, CIN), wn)
-    fill(zn, mixed, dot(flat(h_ref, CIN, 2 * CIN), wn))
-    put(cell_s, cell_hbm, 3, mixed)
-
-    back = gather(
-        [
-            square(zs, b, True)
-            + g_s[:, :, 3 * C + b * LANES : 3 * C + (b + 1) * LANES].astype(F32)
-            for b in range(BLOCKS)
-        ]
-    )
+
+    half = C // 2
+    older_rows = rows_of(xo_s, 0, CIN, 0)
+    newer_rows = rows_of(xn_s, 0, CIN, CIN)
+    newer_parts = []
+    older_parts = []
+    for n in range(2):
+        both = dot(older_rows, wo_ref[:, n * half : (n + 1) * half]) * UNSCALE
+        fill_all(zo.at[2 * n : 2 * n + 2], both)
+        for b in (2 * n, 2 * n + 1):
+            same = g_s[:, :, 3 * C + b * LANES : 3 * C + (b + 1) * LANES].astype(F32)
+            newer_parts.append((square(zs, b, True) + same) * UNSCALE)
+    mixed = []
+    for n in range(2):
+        both = dot(newer_rows, wn_ref[:, n * half : (n + 1) * half]) * UNSCALE
+        fill_all(zn.at[2 * n : 2 * n + 2], both)
+        mixed.append(both[: WIDE * 16].astype(BF16))
+        for b in (2 * n, 2 * n + 1):
+            older_parts.append((column(zc, b, True) + pool(zp, b)) * UNSCALE)
+    put(cell_s, cell_hbm, 3, jnp.concatenate(mixed, axis=1))
+
+    def grad_block(back, w_ref, x_s, stage, hbm, j):
+        term = dot_t(back, w_ref[j * C : (j + 1) * C, :])
+        positive = flat(x_s, j * C, (j + 1) * C).astype(F32) > 0
+        put(stage, hbm, j, jnp.where(positive, term, 0.0))
+
+    column_pre = []
+    square_pre = []
+    pooled = []
+    back = gather(newer_parts)
     for j in range(4):
-        term = dot_t(back, wn_ref[j * C : (j + 1) * C, :])
-        put(ng_s, ng_hbm, j, jnp.where(flat(xn_s, j * C, (j + 1) * C).astype(F32) > 0, term, 0.0))
-    back = gather([column(zc, b, True) + pool(zp, b) for b in range(BLOCKS)])
+        grad_block(back, wn_ref, xn_s, ng_s, ng_hbm, j)
+        column_pre.append(column(zo, j, False, UNSCALE))
+        pooled.append(pool(zo, j))
+    put(cell_s, cell_hbm, 2, gather(pooled))
+    back = gather(older_parts)
     for j in range(4):
-        term = dot_t(back, wo_ref[j * C : (j + 1) * C, :])
-        put(og_s, og_hbm, j, jnp.where(flat(xo_s, j * C, (j + 1) * C).astype(F32) > 0, term, 0.0))
-    put(cell_s, cell_hbm, 0, dot(gather([square(zn, b, False) for b in range(BLOCKS)]), ps))
-    put(cell_s, cell_hbm, 1, dot(gather([column(zo, b, False) for b in range(BLOCKS)]), pc))
-    put(cell_s, cell_hbm, 2, gather([pool(zo, b) for b in range(BLOCKS)]))
+        grad_block(back, wo_ref, xo_s, og_s, og_hbm, j)
+        square_pre.append(square(zn, j, False, UNSCALE))
+    put(cell_s, cell_hbm, 1, dot(gather(column_pre), pc))
+    put(cell_s, cell_hbm, 0, dot(gather(square_pre), ps))
     for copy in copies:
         copy.wait()
 
@@ -236,7 +258,7 @@
     full = lax.all_gather(shard, "rows", axis=0, tiled=False)
 
     def part(lo, hi):
-        piece = (full[:, lo:hi].astype(F32) * (1.0 / SCALE)).astype(BF16)
+        piece = full[:, lo:hi].astype(BF16)
         return piece.reshape(-1, C)
 
     k = older_weight.shape[0]

time: 56.9 us -> 56.1 us (0.986)
  Pallas kernels: 7.86 us -> 7.26 us
    pallas_call x1, Pallas kernels: 5.7 us -> 5.11 us  [run_cell(): pl.pallas_call(cell_kernel, out_shape=(out, out, out), in_specs=[pl.Block...]
  transfers between devices with their start and end apart: 1 -> 1, of which waited for: 0 -> 0; matrix products, arithmetic and copies ran while one was open for 3% -> 2% of each run, Pallas kernels for 0% -> 0%
where the time goes in v2:
time: 56.1 us; the launch traced here: 55.9 us
  blocking collectives  37.8 us (67%)
  starting transfers between devices  8.75 us (16%)
  Pallas kernels  7.26 us (13%)
  other arithmetic  1.36 us (2%)
  between operations  0.71 us (1%)
    all_gather x1, blocking collectives, local(): full = lax.all_gather(shard, 'rows', axis=0, tiled=False)  37.8 us
    ppermute x1, starting transfers between devices, local(): rim = lax.ppermute(rim, 'rows', [(i, i ^ 1) for i in range(count)])  8.75 us
    pallas_call x1, Pallas kernels, run_cell(): pl.pallas_call(cell_kernel, out_shape=(out, out, out), in_specs=[pl.Block...  5.11 us
    pallas_call x1, Pallas kernels, run_halo(): pl.pallas_call(halo_kernel, out_shape=(padded,) * 3 + (pltpu.VMEM((WIDE,...  2.16 us
    convert_element_type x2, other arithmetic, part(): piece = full[:, lo:hi].astype(BF16)  1.3 us
  transfers between devices with their start and end apart: 1, of which 0 were waited for; matrix products, arithmetic and copies ran while one was open for 2% of the time, Pallas kernels for 0%

profile of v2, /device:TPU:1, one launch (start us, length us, event | category | flops | bytes accessed | tf_op | source)
XLA Modules:
  0.0 55.9 jit_solution(13958117314562443988)
XLA Ops:
  0.6 2.2 %halo.1 = (bf16[12,16,2048]{2,1,0:T(8,128)(2,1)S(1)}, bf16[12,16,2048]{2,1,0:T(8,128)(2,1)S(1)}, bf16[12,16,2048]{2,1,0:T(8,128)(2,1)S(1)}, bf16[12,8,6144]{2,1,0:T(8,128)(2,1)S(1)}, bf16[320,512]{1,0:T(8,128)(2,1)S(1)}) custom-call(s32[1]{0:T(128)} %bitcast.core_ref, bf16[12,15,2048]{2,1,0:T(8,128)(2,1)} %bitcast.18, bf16[12,15,2048]{2,1,0:T(8,128)(2,1)} %bitcast.19, ...), custom_call_target="tpu_custom_call" | custom-call | tf_op jit(solution)/shard_map/halo/pallas_call | solution.py:200
  2.8 8.7 %collective-permute-start = (bf16[12,8,6144]{2,1,0:T(8,128)(2,1)S(1)}, bf16[12,8,6144]{2,1,0:T(8,128)(2,1)S(1)}, u32[]{:S(2)}, u32[]{:S(2)}) collective-permute-start(bf16[12,8,6144]{2,1,0:T(8,128)(2,1)S(1)} %get-tuple-element.14), channel_id=1, source_target_pairs={{0,1},{1,0},{2,3},{3,2},{4,5},{5,4},{6,7},{7,6},{8,9},{9,8},{10,11... | collective-permute-start | bytes 3538952 | tf_op jit(solution)/shard_map/ppermute | solution.py:256
  11.6 0.1 multiply_convert_fusion
  11.6 37.8 %all-gather.2 = f16[5120,512]{1,0:T(8,128)(2,1)S(1)} all-gather(f16[320,512]{1,0:T(8,128)(2,1)S(1)} %multiply_convert_fusion), channel_id=2, replica_groups=mesh['dp'=32,'rows'=16] {'rows'}, dimensions={0}, use_global_device_ids=true | all-gather | bytes 5570560 | tf_op jit(solution)/shard_map/all_gather | solution.py:258
  49.4 0.2 slice_convert_fusion.2
  49.7 0.0 copy-start
  49.7 0.0 copy-start.1
  49.7 1.1 %slice_convert_fusion = (bf16[16,128,512]{2,1,0:T(8,128)(2,1)S(1)}, bf16[16,128,512]{2,1,0:T(8,128)(2,1)S(1)}) fusion(f16[16,320,512]{2,1,0:T(8,128)(2,1)S(1)} %bitcast.17), kind=kLoop, calls=%fused_computation | loop fusion | flops 2097152 | bytes 8388608 | tf_op jit(solution)/shard_map/convert_element_type | solution.py:261
  50.8 0.0 collective-permute-done.h_ref
  50.8 0.0 copy-done
  50.8 0.0 copy-done.1
  50.8 5.1 %cell.1 = (bf16[12,15,2048]{2,1,0:T(8,128)(2,1)}, bf16[12,15,2048]{2,1,0:T(8,128)(2,1)}, bf16[12,15,2048]{2,1,0:T(8,128)(2,1)}) custom-call(s32[1]{0:T(128)} %bitcast.core_ref, bf16[12,16,2048]{2,1,0:T(8,128)(2,1)S(1)} %get-tuple-element.11.xo_s, bf16[12,16,2048]{2,1,0:T(8,128)(2,1)S(1)} %get-tuple-element.12.xn_s, ...), custom_call_target="tpu_custom_call" | custom-call | tf_op jit(solution)/shard_map/cell/pallas_call | solution.py:221
Async XLA Ops:
  2.8 48.0 %collective-permute-start = (bf16[12,8,6144]{2,1,0:T(8,128)(2,1)S(1)}, bf16[12,8,6144]{2,1,0:T(8,128)(2,1)S(1)}, u32[]{:S(2)}, u32[]{:S(2)}) collective-permute-start(bf16[12,8,6144]{2,1,0:T(8,128)(2,1)S(1)} %get-tuple-element.14), channel_id=1, source_target_pairs={{0,1},{1,0},{2,3},{3,2},{4,5},{5,4},{6,7},{7,6},{8,9},{9,8},{10,11... | collective-permute-start | bytes 3538952 | tf_op jit(solution)/shard_map/ppermute | solution.py:256
  49.7 1.1 %copy-start = (f32[3,3,512]{2,1,0:T(4,128)S(1)}, f32[3,3,512]{2,1,0:T(4,128)}, u32[]{:S(2)}) copy-start(f32[3,3,512]{2,1,0:T(4,128)} %ks_ref.1) | copy-start | bytes 55300
  49.7 1.1 %copy-start.1 = (f32[7,512]{1,0:T(8,128)S(1)}, f32[7,512]{1,0:T(8,128)}, u32[]{:S(2)}) copy-start(f32[7,512]{1,0:T(8,128)} %kc_ref.1) | copy-start | bytes 43012

commit v3 on v2

--- a/solution.py
+++ b/solution.py
@@ -62,7 +62,7 @@
 
 
 def cell_kernel(
-    core_ref, xo_s, xn_s, g_s, h_ref, wo_ref, wn_ref, ps_ref, pc_ref, ks_ref, kc_ref,
+    core_ref, xo_s, xn_s, g_s, h_ref, w_ref, ks_ref, kc_ref,
     cell_hbm, og_hbm, ng_hbm,
     zo, zn, zs, zc, zp, cell_s, og_s, ng_s, sems,
 ):
@@ -138,8 +138,19 @@
     def rows_of(ref, lo, hi, halo_lo):
         return jnp.concatenate([flat(ref, lo, hi), flat(h_ref, halo_lo, halo_lo + hi - lo)], axis=0)
 
-    ps = ps_ref[...]
-    pc = pc_ref[...]
+    shards = w_ref.shape[0]
+    deep = CIN // shards
+    flatter = C // shards
+
+    def weight(at, lo, hi, first_row=0, last_row=CIN):
+        pieces = range(first_row // deep, last_row // deep)
+        return jnp.concatenate([w_ref[s, at : at + deep, lo:hi] for s in pieces], axis=0)
+
+    def point(at):
+        return jnp.concatenate([w_ref[s, at : at + flatter, :] for s in range(shards)], axis=0)
+
+    ps = point(2 * deep)
+    pc = point(2 * deep + flatter)
     fill_all(zs, dot_t(rows_of(g_s, 0, C, 2 * CIN), ps) * UNSCALE)
     fill_all(zc, dot_t(rows_of(g_s, C, 2 * C, 2 * CIN + C), pc) * UNSCALE)
     fill(zp, flat(g_s, 2 * C, 3 * C), flat(h_ref, 2 * CIN + 2 * C, 2 * CIN + 3 * C))
@@ -149,38 +160,53 @@
     newer_rows = rows_of(xn_s, 0, CIN, CIN)
     newer_parts = []
     older_parts = []
-    for n in range(2):
-        both = dot(older_rows, wo_ref[:, n * half : (n + 1) * half]) * UNSCALE
-        fill_all(zo.at[2 * n : 2 * n + 2], both)
-        for b in (2 * n, 2 * n + 1):
-            same = g_s[:, :, 3 * C + b * LANES : 3 * C + (b + 1) * LANES].astype(F32)
-            newer_parts.append((square(zs, b, True) + same) * UNSCALE)
-    mixed = []
-    for n in range(2):
-        both = dot(newer_rows, wn_ref[:, n * half : (n + 1) * half]) * UNSCALE
-        fill_all(zn.at[2 * n : 2 * n + 2], both)
-        mixed.append(both[: WIDE * 16].astype(BF16))
-        for b in (2 * n, 2 * n + 1):
-            older_parts.append((column(zc, b, True) + pool(zp, b)) * UNSCALE)
-    put(cell_s, cell_hbm, 3, jnp.concatenate(mixed, axis=1))
-
-    def grad_block(back, w_ref, x_s, stage, hbm, j):
-        term = dot_t(back, w_ref[j * C : (j + 1) * C, :])
-        positive = flat(x_s, j * C, (j + 1) * C).astype(F32) > 0
-        put(stage, hbm, j, jnp.where(positive, term, 0.0))
-
     column_pre = []
     square_pre = []
     pooled = []
+    mixed = []
+
+    def newer_part(b):
+        same = g_s[:, :, 3 * C + b * LANES : 3 * C + (b + 1) * LANES].astype(F32)
+        newer_parts.append((square(zs, b, True) + same) * UNSCALE)
+
+    def older_part(b):
+        older_parts.append((column(zc, b, True) + pool(zp, b)) * UNSCALE)
+
+    def older_half(n):
+        both = dot(older_rows, weight(0, n * half, (n + 1) * half)) * UNSCALE
+        fill_all(zo.at[2 * n : 2 * n + 2], both)
+
+    def newer_half(n):
+        both = dot(newer_rows, weight(deep, n * half, (n + 1) * half)) * UNSCALE
+        fill_all(zn.at[2 * n : 2 * n + 2], both)
+        mixed.append(both[: WIDE * 16].astype(BF16))
+
+    def forward_older(b):
+        column_pre.append(column(zo, b, False, UNSCALE))
+        pooled.append(pool(zo, b))
+
+    def grad_block(back, at, x_s, stage, hbm, j):
+        term = dot_t(back, weight(at, 0, C, j * C, (j + 1) * C)).astype(BF16)
+        positive = flat(x_s, j * C, (j + 1) * C) > 0
+        put(stage, hbm, j, jnp.where(positive, term, jnp.zeros_like(term)))
+
+    for n in range(2):
+        older_half(n)
+        newer_part(2 * n)
+        newer_part(2 * n + 1)
+    for n in range(2):
+        newer_half(n)
+        older_part(2 * n)
+        older_part(2 * n + 1)
+    put(cell_s, cell_hbm, 3, jnp.concatenate(mixed, axis=1))
     back = gather(newer_parts)
     for j in range(4):
-        grad_block(back, wn_ref, xn_s, ng_s, ng_hbm, j)
-        column_pre.append(column(zo, j, False, UNSCALE))
-        pooled.append(pool(zo, j))
+        grad_block(back, deep, xn_s, ng_s, ng_hbm, j)
+        forward_older(j)
     put(cell_s, cell_hbm, 2, gather(pooled))
     back = gather(older_parts)
     for j in range(4):
-        grad_block(back, wo_ref, xo_s, og_s, og_hbm, j)
+        grad_block(back, 0, xo_s, og_s, og_hbm, j)
         square_pre.append(square(zn, j, False, UNSCALE))
     put(cell_s, cell_hbm, 1, dot(gather(column_pre), pc))
     put(cell_s, cell_hbm, 0, dot(gather(square_pre), ps))
@@ -221,7 +247,7 @@
     return pl.pallas_call(
         cell_kernel,
         out_shape=(out, out, out),
-        in_specs=[pl.BlockSpec(memory_space=pltpu.SMEM)] + [vmem] * 10,
+        in_specs=[pl.BlockSpec(memory_space=pltpu.SMEM)] + [vmem] * 7,
         out_specs=(pl.BlockSpec(memory_space=pl.ANY),) * 3,
         scratch_shapes=[field] * 5 + [stage] * 3 + [pltpu.SemaphoreType.DMA((12,))],
         compiler_params=pltpu.CompilerParams(vmem_limit_bytes=24 * 1024 * 1024),
@@ -255,24 +281,15 @@
     )
     rim = lax.ppermute(rim, "rows", [(i, i ^ 1) for i in range(count)])
     shard = (shard * jnp.asarray(SCALE, BF16)).astype(jnp.float16)
-    full = lax.all_gather(shard, "rows", axis=0, tiled=False)
-
-    def part(lo, hi):
-        piece = full[:, lo:hi].astype(BF16)
-        return piece.reshape(-1, C)
-
-    k = older_weight.shape[0]
-    p = square_point.shape[0]
+    full = lax.all_gather(shard, "rows", axis=0, tiled=False).astype(BF16)
+
     cell, og, ng = run_cell(
         core,
         xo,
         xn,
         grad,
         rim,
-        part(0, k),
-        part(k, 2 * k),
-        part(2 * k, 2 * k + p),
-        part(2 * k + p, 2 * k + 2 * p),
+        full,
         square_kernel,
         column_kernel,
     )

time: 56.1 us -> 55.4 us (0.988)
    convert_element_type x2 -> x1, other arithmetic: 1.3 us -> 1.07 us  [local(): full = lax.all_gather(shard, 'rows', axis=0, tiled=False).astype(BF16)]
where the time goes in v3:
time: 55.4 us; the launch traced here: 55.2 us
  blocking collectives  37.8 us (68%)
  starting transfers between devices  8.75 us (16%)
  Pallas kernels  6.8 us (12%)
  other arithmetic  1.14 us (2%)
  between operations  0.69 us (1%)
    all_gather x1, blocking collectives, local(): full = lax.all_gather(shard, 'rows', axis=0, tiled=False).astype(BF16)  37.8 us
    ppermute x1, starting transfers between devices, local(): rim = lax.ppermute(rim, 'rows', [(i, i ^ 1) for i in range(count)])  8.75 us
    pallas_call x1, Pallas kernels, run_cell(): pl.pallas_call(cell_kernel, out_shape=(out, out, out), in_specs=[pl.Block...  4.65 us
    pallas_call x1, Pallas kernels, run_halo(): pl.pallas_call(halo_kernel, out_shape=(padded,) * 3 + (pltpu.VMEM((WIDE,...  2.15 us
  transfers between devices with their start and end apart: 1, of which 0 were waited for; matrix products, arithmetic and copies ran while one was open for 2% of the time, Pallas kernels for 0%

profile of v3, /device:TPU:1, one launch (start us, length us, event | category | flops | bytes accessed | tf_op | source)
XLA Modules:
  0.0 55.2 jit_solution(14857031244009269291)
XLA Ops:
  0.6 2.2 %halo.1 = (bf16[12,16,2048]{2,1,0:T(8,128)(2,1)S(1)}, bf16[12,16,2048]{2,1,0:T(8,128)(2,1)S(1)}, bf16[12,16,2048]{2,1,0:T(8,128)(2,1)S(1)}, bf16[12,8,6144]{2,1,0:T(8,128)(2,1)S(1)}, bf16[320,512]{1,0:T(8,128)(2,1)S(1)}) custom-call(s32[1]{0:T(128)} %bitcast.core_ref, bf16[12,15,2048]{2,1,0:T(8,128)(2,1)} %bitcast.9, bf16[12,15,2048]{2,1,0:T(8,128)(2,1)} %bitcast.10, ...), custom_call_target="tpu_custom_call" | custom-call | tf_op jit(solution)/shard_map/halo/pallas_call | solution.py:226
  2.8 8.7 %collective-permute-start = (bf16[12,8,6144]{2,1,0:T(8,128)(2,1)S(1)}, bf16[12,8,6144]{2,1,0:T(8,128)(2,1)S(1)}, u32[]{:S(2)}, u32[]{:S(2)}) collective-permute-start(bf16[12,8,6144]{2,1,0:T(8,128)(2,1)S(1)} %get-tuple-element.14), channel_id=1, source_target_pairs={{0,1},{1,0},{2,3},{3,2},{4,5},{5,4},{6,7},{7,6},{8,9},{9,8},{10,11... | collective-permute-start | bytes 3538952 | tf_op jit(solution)/shard_map/ppermute | solution.py:282
  11.6 0.1 multiply_convert_fusion
  11.6 37.8 %all-gather.2 = f16[5120,512]{1,0:T(8,128)(2,1)S(1)} all-gather(f16[320,512]{1,0:T(8,128)(2,1)S(1)} %multiply_convert_fusion), channel_id=2, replica_groups=mesh['dp'=32,'rows'=16] {'rows'}, dimensions={0}, use_global_device_ids=true | all-gather | bytes 5570560 | tf_op jit(solution)/shard_map/all_gather | solution.py:284
  49.4 0.0 copy-start
  49.4 0.0 copy-start.1
  49.5 1.1 %convert_element_type.8 = bf16[5120,512]{1,0:T(8,128)(2,1)S(1)} convert(f16[5120,512]{1,0:T(8,128)(2,1)S(1)} %all-gather.2) | non-fusion elementwise | flops 2621440 | bytes 10485760 | tf_op jit(solution)/shard_map/convert_element_type | solution.py:284
  50.5 0.0 collective-permute-done.h_ref
  50.5 0.0 copy-done
  50.5 0.0 copy-done.1
  50.6 4.6 %cell.1 = (bf16[12,15,2048]{2,1,0:T(8,128)(2,1)}, bf16[12,15,2048]{2,1,0:T(8,128)(2,1)}, bf16[12,15,2048]{2,1,0:T(8,128)(2,1)}) custom-call(s32[1]{0:T(128)} %bitcast.core_ref, bf16[12,16,2048]{2,1,0:T(8,128)(2,1)S(1)} %get-tuple-element.11.xo_s, bf16[12,16,2048]{2,1,0:T(8,128)(2,1)S(1)} %get-tuple-element.12.xn_s, ...), custom_call_target="tpu_custom_call" | custom-call | tf_op jit(solution)/shard_map/cell/pallas_call | solution.py:247
Async XLA Ops:
  2.8 47.7 %collective-permute-start = (bf16[12,8,6144]{2,1,0:T(8,128)(2,1)S(1)}, bf16[12,8,6144]{2,1,0:T(8,128)(2,1)S(1)}, u32[]{:S(2)}, u32[]{:S(2)}) collective-permute-start(bf16[12,8,6144]{2,1,0:T(8,128)(2,1)S(1)} %get-tuple-element.14), channel_id=1, source_target_pairs={{0,1},{1,0},{2,3},{3,2},{4,5},{5,4},{6,7},{7,6},{8,9},{9,8},{10,11... | collective-permute-start | bytes 3538952 | tf_op jit(solution)/shard_map/ppermute | solution.py:282
  49.4 1.1 %copy-start = (f32[3,3,512]{2,1,0:T(4,128)S(1)}, f32[3,3,512]{2,1,0:T(4,128)}, u32[]{:S(2)}) copy-start(f32[3,3,512]{2,1,0:T(4,128)} %ks_ref.1) | copy-start | bytes 55300
  49.4 1.1 %copy-start.1 = (f32[7,512]{1,0:T(8,128)S(1)}, f32[7,512]{1,0:T(8,128)}, u32[]{:S(2)}) copy-start(f32[7,512]{1,0:T(8,128)} %kc_ref.1) | copy-start | bytes 43012

commit v4 on v3

--- a/solution.py
+++ b/solution.py
@@ -13,7 +13,9 @@
 ROWS = 15
 LANES = 128
 BLOCKS = C // LANES
-PIECES = 4
+PIECES = 1
+OWN = WIDE * 16
+FAR = WIDE * 8
 SCALE = 2.0**17
 UNSCALE = 1.0 / SCALE
 
@@ -33,6 +35,15 @@
 ):
     first = core_ref[0] == 0
     turn = jnp.where(first, 1, 7)
+
+    def far(rows):
+        return rows.reshape(FAR, rows.shape[2]).astype(BF16)
+
+    def near(rows):
+        last = lax.broadcasted_iota(jnp.int32, rows.shape, 1) == 7
+        both = jnp.concatenate([jnp.zeros_like(rows), jnp.where(last, rows, 0.0)], axis=1)
+        return both.reshape(OWN, rows.shape[2]).astype(BF16)
+
     fields = ((xo_hbm, xo_out, True), (xn_hbm, xn_out, True), (g_hbm, g_out, False))
     copies = []
     for at, (src, _, _) in enumerate(fields):
@@ -55,8 +66,19 @@
             copies[at * PIECES + q].wait()
         v = raw[at]
         dst[:, 0:ROWS, :] = jnp.maximum(v, 0) if relu else v
-        sent = jnp.where(first, dst[:, 8:16, :].astype(F32), dst[:, 0:8, :].astype(F32))
-        h_out[:, :, at * CIN : (at + 1) * CIN] = pltpu.roll(sent, turn, 1).astype(BF16)
+        width = 3 * C if at == 2 else CIN
+        sent = jnp.where(
+            first, dst[:, 8:16, :width].astype(F32), dst[:, 0:8, :width].astype(F32)
+        )
+        sent = pltpu.roll(sent, turn, 1)
+        if at == 0:
+            h_out[0:FAR, :] = far(sent)
+        elif at == 1:
+            h_out[FAR : FAR + OWN, :] = near(sent)
+        else:
+            h_out[FAR + OWN :, 0:C] = near(sent[:, :, 0:C])
+            h_out[FAR + OWN : FAR + OWN + FAR, C : 2 * C] = far(sent[:, :, C : 2 * C])
+            h_out[FAR + OWN :, 2 * C : 3 * C] = near(sent[:, :, 2 * C : 3 * C])
     for copy in loads:
         copy.wait()
 
@@ -71,6 +93,8 @@
     above = jnp.where((slot >= 5) & jnp.logical_not(first), 1.0, 0.0).astype(F32)
     below = jnp.where((slot < 2) & first, 1.0, 0.0).astype(F32)
     edge = jnp.where((slot == 7) & first, 1.0, 0.0).astype(F32)
+    before = jnp.where((slot == 7) & jnp.logical_not(first), 1.0, 0.0).astype(F32)
+    after = jnp.where((slot < 7) | first, 1.0, 0.0).astype(F32)
 
     for z in (zo, zn, zs, zp):
         z[:, 0] = jnp.zeros((BLOCKS, 32, LANES), F32)
@@ -88,7 +112,16 @@
             z[b, 1 : WIDE + 1, 24:32, :] = h * below
 
     def fill_all(z, both):
-        fill(z, both[: WIDE * 16], both[WIDE * 16 :])
+        fill(z, both[:OWN], both[OWN:])
+
+    def fill_near(z, own):
+        own = own.astype(BF16).astype(F32).reshape(WIDE, 16, -1)
+        for b in range(own.shape[2] // LANES):
+            o = own[:, :, b * LANES : (b + 1) * LANES]
+            z[b, 1 : WIDE + 1, 0:8, :] = o[:, 8:16] * before
+            z[b, 1 : WIDE + 1, 8:16, :] = o[:, 0:8]
+            z[b, 1 : WIDE + 1, 16:24, :] = o[:, 8:16] * after
+            z[b, 1 : WIDE + 1, 24:32, :] = jnp.zeros((WIDE, 8, LANES), F32)
 
     def column(z, b, flip, scale=None):
         acc = None
@@ -135,8 +168,11 @@
         v = ref[:, :, lo:hi]
         return v.reshape(-1, hi - lo)
 
-    def rows_of(ref, lo, hi, halo_lo):
-        return jnp.concatenate([flat(ref, lo, hi), flat(h_ref, halo_lo, halo_lo + hi - lo)], axis=0)
+    def with_far(own, rows, lo):
+        return jnp.concatenate([own, h_ref[rows : rows + FAR, lo : lo + own.shape[1]]], axis=0)
+
+    def with_near(own, rows, lo):
+        return own + h_ref[rows : rows + OWN, lo : lo + own.shape[1]]
 
     shards = w_ref.shape[0]
     deep = CIN // shards
@@ -151,13 +187,14 @@
 
     ps = point(2 * deep)
     pc = point(2 * deep + flatter)
-    fill_all(zs, dot_t(rows_of(g_s, 0, C, 2 * CIN), ps) * UNSCALE)
-    fill_all(zc, dot_t(rows_of(g_s, C, 2 * C, 2 * CIN + C), pc) * UNSCALE)
-    fill(zp, flat(g_s, 2 * C, 3 * C), flat(h_ref, 2 * CIN + 2 * C, 2 * CIN + 3 * C))
+    base = FAR + OWN
+    fill_near(zs, dot_t(with_near(flat(g_s, 0, C), base, 0), ps) * UNSCALE)
+    fill_all(zc, dot_t(with_far(flat(g_s, C, 2 * C), base, C), pc) * UNSCALE)
+    fill_near(zp, with_near(flat(g_s, 2 * C, 3 * C), base, 2 * C))
 
     half = C // 2
-    older_rows = rows_of(xo_s, 0, CIN, 0)
-    newer_rows = rows_of(xn_s, 0, CIN, CIN)
+    older_rows = with_far(flat(xo_s, 0, CIN), 0, 0)
+    newer_rows = with_near(flat(xn_s, 0, CIN), FAR, 0)
     newer_parts = []
     older_parts = []
     column_pre = []
@@ -178,8 +215,8 @@
 
     def newer_half(n):
         both = dot(newer_rows, weight(deep, n * half, (n + 1) * half)) * UNSCALE
-        fill_all(zn.at[2 * n : 2 * n + 2], both)
-        mixed.append(both[: WIDE * 16].astype(BF16))
+        fill_near(zn.at[2 * n : 2 * n + 2], both)
+        mixed.append(both.astype(BF16))
 
     def forward_older(b):
         column_pre.append(column(zo, b, False, UNSCALE))
@@ -226,7 +263,7 @@
     return pl.pallas_call(
         halo_kernel,
         out_shape=(padded,) * 3
-        + (pltpu.VMEM((WIDE, 8, 3 * CIN), BF16), pltpu.VMEM((shards, C), BF16)),
+        + (pltpu.VMEM((FAR + 2 * OWN, CIN), BF16), pltpu.VMEM((shards, C), BF16)),
         in_specs=[pl.BlockSpec(memory_space=pltpu.SMEM)] + [hbm] * 7,
         out_specs=(vmem,) * 5,
         scratch_shapes=[

time: 55.4 us -> 55.2 us (level)
  no operation moved by 1% of the time
where the time goes in v4:
time: 55.2 us; the launch traced here: 55.1 us
  blocking collectives  37.8 us (68%)
  starting transfers between devices  8.75 us (16%)
  Pallas kernels  6.66 us (12%)
  other arithmetic  1.14 us (2%)
  between operations  0.69 us (1%)
    all_gather x1, blocking collectives, local(): full = lax.all_gather(shard, 'rows', axis=0, tiled=False).astype(BF16)  37.8 us
    ppermute x1, starting transfers between devices, local(): rim = lax.ppermute(rim, 'rows', [(i, i ^ 1) for i in range(count)])  8.75 us
    pallas_call x1, Pallas kernels, run_cell(): pl.pallas_call(cell_kernel, out_shape=(out, out, out), in_specs=[pl.Block...  4.55 us
    pallas_call x1, Pallas kernels, run_halo(): pl.pallas_call(halo_kernel, out_shape=(padded,) * 3 + (pltpu.VMEM((FAR +...  2.11 us
  transfers between devices with their start and end apart: 1, of which 0 were waited for; matrix products, arithmetic and copies ran while one was open for 2% of the time, Pallas kernels for 0%

profile of v4, /device:TPU:1, one launch (start us, length us, event | category | flops | bytes accessed | tf_op | source)
XLA Modules:
  0.0 55.1 jit_solution(237287039098352565)
XLA Ops:
  0.6 2.1 %halo.1 = (bf16[12,16,2048]{2,1,0:T(8,128)(2,1)S(1)}, bf16[12,16,2048]{2,1,0:T(8,128)(2,1)S(1)}, bf16[12,16,2048]{2,1,0:T(8,128)(2,1)S(1)}, bf16[480,2048]{1,0:T(8,128)(2,1)S(1)}, bf16[320,512]{1,0:T(8,128)(2,1)S(1)}) custom-call(s32[1]{0:T(128)} %bitcast.core_ref, bf16[12,15,2048]{2,1,0:T(8,128)(2,1)} %bitcast.9, bf16[12,15,2048]{2,1,0:T(8,128)(2,1)} %bitcast.10, ...), custom_call_target="tpu_custom_call" | custom-call | tf_op jit(solution)/shard_map/halo/pallas_call | solution.py:263
  2.8 8.7 %collective-permute-start = (bf16[480,2048]{1,0:T(8,128)(2,1)S(1)}, bf16[480,2048]{1,0:T(8,128)(2,1)S(1)}, u32[]{:S(2)}, u32[]{:S(2)}) collective-permute-start(bf16[480,2048]{1,0:T(8,128)(2,1)S(1)} %get-tuple-element.14), channel_id=1, source_target_pairs={{0,1},{1,0},{2,3},{3,2},{4,5},{5,4},{6,7},{7,6},{8,9},{9,8},{10,11... | collective-permute-start | bytes 5898248 | tf_op jit(solution)/shard_map/ppermute | solution.py:319
  11.5 0.1 multiply_convert_fusion
  11.6 37.8 %all-gather.2 = f16[5120,512]{1,0:T(8,128)(2,1)S(1)} all-gather(f16[320,512]{1,0:T(8,128)(2,1)S(1)} %multiply_convert_fusion), channel_id=2, replica_groups=mesh['dp'=32,'rows'=16] {'rows'}, dimensions={0}, use_global_device_ids=true | all-gather | bytes 5570560 | tf_op jit(solution)/shard_map/all_gather | solution.py:321
  49.4 0.0 copy-start
  49.4 0.0 copy-start.1
  49.4 1.1 %convert_element_type.8 = bf16[5120,512]{1,0:T(8,128)(2,1)S(1)} convert(f16[5120,512]{1,0:T(8,128)(2,1)S(1)} %all-gather.2) | non-fusion elementwise | flops 2621440 | bytes 10485760 | tf_op jit(solution)/shard_map/convert_element_type | solution.py:321
  50.5 0.0 collective-permute-done.h_ref
  50.5 0.0 copy-done
  50.5 0.0 copy-done.1
  50.5 4.6 %cell.1 = (bf16[12,15,2048]{2,1,0:T(8,128)(2,1)}, bf16[12,15,2048]{2,1,0:T(8,128)(2,1)}, bf16[12,15,2048]{2,1,0:T(8,128)(2,1)}) custom-call(s32[1]{0:T(128)} %bitcast.core_ref, bf16[12,16,2048]{2,1,0:T(8,128)(2,1)S(1)} %get-tuple-element.11.xo_s, bf16[12,16,2048]{2,1,0:T(8,128)(2,1)S(1)} %get-tuple-element.12.xn_s, ...), custom_call_target="tpu_custom_call" | custom-call | tf_op jit(solution)/shard_map/cell/pallas_call | solution.py:284
Async XLA Ops:
  2.8 47.7 %collective-permute-start = (bf16[480,2048]{1,0:T(8,128)(2,1)S(1)}, bf16[480,2048]{1,0:T(8,128)(2,1)S(1)}, u32[]{:S(2)}, u32[]{:S(2)}) collective-permute-start(bf16[480,2048]{1,0:T(8,128)(2,1)S(1)} %get-tuple-element.14), channel_id=1, source_target_pairs={{0,1},{1,0},{2,3},{3,2},{4,5},{5,4},{6,7},{7,6},{8,9},{9,8},{10,11... | collective-permute-start | bytes 5898248 | tf_op jit(solution)/shard_map/ppermute | solution.py:319
  49.4 1.1 %copy-start = (f32[3,3,512]{2,1,0:T(4,128)S(1)}, f32[3,3,512]{2,1,0:T(4,128)}, u32[]{:S(2)}) copy-start(f32[3,3,512]{2,1,0:T(4,128)} %ks_ref.1) | copy-start | bytes 55300
  49.4 1.1 %copy-start.1 = (f32[7,512]{1,0:T(8,128)S(1)}, f32[7,512]{1,0:T(8,128)}, u32[]{:S(2)}) copy-start(f32[7,512]{1,0:T(8,128)} %kc_ref.1) | copy-start | bytes 43012

commit v5 on v4

--- a/solution.py
+++ b/solution.py
@@ -223,7 +223,7 @@
         pooled.append(pool(zo, b))
 
     def grad_block(back, at, x_s, stage, hbm, j):
-        term = dot_t(back, weight(at, 0, C, j * C, (j + 1) * C)).astype(BF16)
+        term = dot_t(weight(at, 0, C, j * C, (j + 1) * C), back).astype(BF16).T
         positive = flat(x_s, j * C, (j + 1) * C) > 0
         put(stage, hbm, j, jnp.where(positive, term, jnp.zeros_like(term)))
 
@@ -246,7 +246,16 @@
         grad_block(back, 0, xo_s, og_s, og_hbm, j)
         square_pre.append(square(zn, j, False, UNSCALE))
     put(cell_s, cell_hbm, 1, dot(gather(column_pre), pc))
-    put(cell_s, cell_hbm, 0, dot(gather(square_pre), ps))
+    pre = gather(square_pre)
+    for n in range(2):
+        lanes = pl.ds(n * half, half)
+        value = dot(pre, ps[:, n * half : (n + 1) * half]).astype(BF16)
+        cell_s[0, :, :, lanes] = value.reshape(WIDE, 16, half)[:, 0:ROWS, :]
+        copy = pltpu.make_async_copy(
+            cell_s.at[0, :, :, lanes], cell_hbm.at[:, :, lanes], sems.at[len(copies)]
+        )
+        copy.start()
+        copies.append(copy)
     for copy in copies:
         copy.wait()
 
@@ -286,7 +295,7 @@
         out_shape=(out, out, out),
         in_specs=[pl.BlockSpec(memory_space=pltpu.SMEM)] + [vmem] * 7,
         out_specs=(pl.BlockSpec(memory_space=pl.ANY),) * 3,
-        scratch_shapes=[field] * 5 + [stage] * 3 + [pltpu.SemaphoreType.DMA((12,))],
+        scratch_shapes=[field] * 5 + [stage] * 3 + [pltpu.SemaphoreType.DMA((13,))],
         compiler_params=pltpu.CompilerParams(vmem_limit_bytes=24 * 1024 * 1024),
         name="cell",
     )(core, *placed(operands, pltpu.VMEM))

time: 55.2 us -> 55.1 us (level)
  no operation moved by 1% of the time
where the time goes in v5:
time: 55.1 us; the launch traced here: 54.9 us
  blocking collectives  37.8 us (69%)
  starting transfers between devices  8.75 us (16%)
  Pallas kernels  6.5 us (12%)
  other arithmetic  1.14 us (2%)
  between operations  0.69 us (1%)
    all_gather x1, blocking collectives, local(): full = lax.all_gather(shard, 'rows', axis=0, tiled=False).astype(BF16)  37.8 us
    ppermute x1, starting transfers between devices, local(): rim = lax.ppermute(rim, 'rows', [(i, i ^ 1) for i in range(count)])  8.75 us
    pallas_call x1, Pallas kernels, run_cell(): pl.pallas_call(cell_kernel, out_shape=(out, out, out), in_specs=[pl.Block...  4.4 us
    pallas_call x1, Pallas kernels, run_halo(): pl.pallas_call(halo_kernel, out_shape=(padded,) * 3 + (pltpu.VMEM((FAR +...  2.11 us
  transfers between devices with their start and end apart: 1, of which 0 were waited for; matrix products, arithmetic and copies ran while one was open for 2% of the time, Pallas kernels for 0%

profile of v5, /device:TPU:1, one launch (start us, length us, event | category | flops | bytes accessed | tf_op | source)
XLA Modules:
  0.0 54.9 jit_solution(15494237508903226551)
XLA Ops:
  0.6 2.1 %halo.1 = (bf16[12,16,2048]{2,1,0:T(8,128)(2,1)S(1)}, bf16[12,16,2048]{2,1,0:T(8,128)(2,1)S(1)}, bf16[12,16,2048]{2,1,0:T(8,128)(2,1)S(1)}, bf16[480,2048]{1,0:T(8,128)(2,1)S(1)}, bf16[320,512]{1,0:T(8,128)(2,1)S(1)}) custom-call(s32[1]{0:T(128)} %bitcast.core_ref, bf16[12,15,2048]{2,1,0:T(8,128)(2,1)} %bitcast.9, bf16[12,15,2048]{2,1,0:T(8,128)(2,1)} %bitcast.10, ...), custom_call_target="tpu_custom_call" | custom-call | tf_op jit(solution)/shard_map/halo/pallas_call | solution.py:272
  2.8 8.7 %collective-permute-start = (bf16[480,2048]{1,0:T(8,128)(2,1)S(1)}, bf16[480,2048]{1,0:T(8,128)(2,1)S(1)}, u32[]{:S(2)}, u32[]{:S(2)}) collective-permute-start(bf16[480,2048]{1,0:T(8,128)(2,1)S(1)} %get-tuple-element.14), channel_id=1, source_target_pairs={{0,1},{1,0},{2,3},{3,2},{4,5},{5,4},{6,7},{7,6},{8,9},{9,8},{10,11... | collective-permute-start | bytes 5898248 | tf_op jit(solution)/shard_map/ppermute | solution.py:328
  11.5 0.1 multiply_convert_fusion
  11.6 37.8 %all-gather.2 = f16[5120,512]{1,0:T(8,128)(2,1)S(1)} all-gather(f16[320,512]{1,0:T(8,128)(2,1)S(1)} %multiply_convert_fusion), channel_id=2, replica_groups=mesh['dp'=32,'rows'=16] {'rows'}, dimensions={0}, use_global_device_ids=true | all-gather | bytes 5570560 | tf_op jit(solution)/shard_map/all_gather | solution.py:330
  49.4 0.0 copy-start
  49.4 0.0 copy-start.1
  49.4 1.1 %convert_element_type.8 = bf16[5120,512]{1,0:T(8,128)(2,1)S(1)} convert(f16[5120,512]{1,0:T(8,128)(2,1)S(1)} %all-gather.2) | non-fusion elementwise | flops 2621440 | bytes 10485760 | tf_op jit(solution)/shard_map/convert_element_type | solution.py:330
  50.5 0.0 collective-permute-done.h_ref
  50.5 0.0 copy-done
  50.5 0.0 copy-done.1
  50.5 4.4 %cell.1 = (bf16[12,15,2048]{2,1,0:T(8,128)(2,1)}, bf16[12,15,2048]{2,1,0:T(8,128)(2,1)}, bf16[12,15,2048]{2,1,0:T(8,128)(2,1)}) custom-call(s32[1]{0:T(128)} %bitcast.core_ref, bf16[12,16,2048]{2,1,0:T(8,128)(2,1)S(1)} %get-tuple-element.11.xo_s, bf16[12,16,2048]{2,1,0:T(8,128)(2,1)S(1)} %get-tuple-element.12.xn_s, ...), custom_call_target="tpu_custom_call" | custom-call | tf_op jit(solution)/shard_map/cell/pallas_call | solution.py:293
Async XLA Ops:
  2.8 47.7 %collective-permute-start = (bf16[480,2048]{1,0:T(8,128)(2,1)S(1)}, bf16[480,2048]{1,0:T(8,128)(2,1)S(1)}, u32[]{:S(2)}, u32[]{:S(2)}) collective-permute-start(bf16[480,2048]{1,0:T(8,128)(2,1)S(1)} %get-tuple-element.14), channel_id=1, source_target_pairs={{0,1},{1,0},{2,3},{3,2},{4,5},{5,4},{6,7},{7,6},{8,9},{9,8},{10,11... | collective-permute-start | bytes 5898248 | tf_op jit(solution)/shard_map/ppermute | solution.py:328
  49.4 1.1 %copy-start = (f32[3,3,512]{2,1,0:T(4,128)S(1)}, f32[3,3,512]{2,1,0:T(4,128)}, u32[]{:S(2)}) copy-start(f32[3,3,512]{2,1,0:T(4,128)} %ks_ref.1) | copy-start | bytes 55300
  49.4 1.1 %copy-start.1 = (f32[7,512]{1,0:T(8,128)S(1)}, f32[7,512]{1,0:T(8,128)}, u32[]{:S(2)}) copy-start(f32[7,512]{1,0:T(8,128)} %kc_ref.1) | copy-start | bytes 43012
